TPU v7x, 512 devices: a whole 4x4x16 slice. The times are simulated.
512 devices in a mesh: docs: 16 (over y, x), supp: 32 (over z, core).
Axes of the slice: x: 4, y: 4, z: 16, core: 2. Of those that a mesh axis runs over, the one named last changes fastest.
Arguments:
- vocab_table: bfloat16 [100000, 300], P('docs'), may hold values from -0.69140625 to 0.69140625
- support_atoms: bfloat16 [65536, 300], P('supp'), may hold values from -0.69140625 to 0.69140625
- weight_logits: float32 [65536], P('supp'), may hold values from -6 to 6
- word_counts: int32 [32], P('docs'), may hold values from 1 to 600, 11520 in all
- word_shard: int32 [20480, 1], P('docs'), may hold values from 0 to 15; in each aligned block of 1280 rows (0 to 1279, 1280 to 2559, ...) at most 128 rows name the same one
- word_row: int32 [20480], P('docs'), may hold values from 0 to 6249
Outputs:
- row_potential: float32 [32, 640], P('docs')
- col_potential: float32 [32, 65536], P('docs', 'supp')
- new_log_weights: float32 [65536], P('supp')
Inputs may be any that keep to these rules, and one draw needn't show every extreme that they name: `word_shard`: within the 1280 word slots of each index of docs (aligned blocks), no shard number appears more than 128 times, and some number appears exactly 128 times. `word_counts`: the longest document has exactly 600 words.
All inputs are finite; a program needn't handle non-finite values. No bound on the sum of `word_counts` on one device may be relied on, other than what follows from the above.
Results may differ from a plain program's by a relative error of at most 0.0003.
Values may be sent and summed in bfloat16 or wider, within the bound.
No kernel may reach another device: no remote copies, remote signals or barrier semaphores. Data moves between devices by JAX's collectives and lax.ppermute only.
A program may use at most 64 MiB of HBM per device.

v0:
```python
import jax
import jax.numpy as jnp
from jax import lax
from jax.sharding import PartitionSpec as P

ITERS = 2


epsilon = 0.05


def extent_supp(largest, summed):
    global_max = lax.pmax(largest, "supp")
    global_sum = lax.psum(summed * jnp.exp(largest - global_max), "supp")
    return global_max + jnp.log(global_sum)


def fetch_rows(requests, vocab_table):
    return lax.all_to_all(
        vocab_table[lax.all_to_all(requests, "docs", split_axis=0, concat_axis=0, tiled=True)],
        "docs",
        split_axis=0,
        concat_axis=0,
        tiled=True,
    )


def shards(vocab_table, support_atoms, weight_logits, word_counts, word_shard, word_row):
    groups = lax.axis_size("docs")
    supp_count = lax.axis_size("supp")
    docs_here = word_counts.shape[0]
    slot_count = word_row.shape[0]
    doc_slots = slot_count // docs_here
    atom_count = support_atoms.shape[0]
    capacity = supp_count * (
        (5 * slot_count + 4 * groups * supp_count - 1) // (4 * groups * supp_count)
    )
    word_owner = word_shard[:, 0]
    member = (word_owner[:, None] == jnp.arange(groups, dtype=jnp.int32)[None, :]).astype(jnp.int32)
    slot_rank = jnp.sum((jnp.cumsum(member, axis=0) - 1) * member, axis=1)
    requests = jnp.zeros((groups, capacity), jnp.int32).at[word_owner, slot_rank].set(word_row)
    fetched = fetch_rows(requests, vocab_table)
    word_vecs = fetched[word_owner, slot_rank]
    words_sq = jnp.sum(jnp.square(word_vecs.astype(jnp.float32)), axis=1).reshape(
        docs_here, doc_slots
    )
    atoms_sq = jnp.sum(jnp.square(support_atoms.astype(jnp.float32)), axis=1)
    product = jnp.dot(word_vecs, support_atoms.T, preferred_element_type=jnp.float32)
    product = product.reshape(docs_here, doc_slots, atom_count)
    stored = words_sq[:, :, None] + atoms_sq[None, None, :] - 2.0 * product
    logit_max = jnp.max(weight_logits)
    logit_sum = jnp.sum(jnp.exp(weight_logits - logit_max))
    log_base = weight_logits - extent_supp(logit_max, logit_sum)
    live_mask = jnp.arange(doc_slots)[None, :] < word_counts[:, None]
    log_share = -epsilon * jnp.log(word_counts.astype(jnp.float32))

    def column_extent(row_pot, dist_grid):
        scores = (row_pot[:, :, None] - dist_grid) / epsilon
        largest = jnp.max(jnp.where(live_mask[:, :, None], scores, -jnp.inf), axis=1)
        summed = jnp.sum(
            jnp.where(live_mask[:, :, None], jnp.exp(scores - largest[:, None, :]), 0.0), axis=1
        )
        return largest + jnp.log(summed)

    row_pot = jnp.zeros((docs_here, doc_slots), jnp.float32)
    col_pot = jnp.zeros((docs_here, atom_count), jnp.float32)
    for sweep in range(ITERS):
        dist_grid = stored
        col_pot = epsilon * log_base[None, :] - epsilon * column_extent(row_pot, dist_grid)
        scores = (col_pot[:, None, :] - dist_grid) / epsilon
        largest = jnp.max(scores, axis=2)
        summed = jnp.sum(jnp.exp(scores - largest[:, :, None]), axis=2)
        row_ext = extent_supp(largest, summed)
        row_pot = jnp.where(live_mask, log_share[:, None] - epsilon * row_ext, 0.0)
    dist_grid = stored
    log_marg = col_pot / epsilon + column_extent(row_pot, dist_grid)
    grand_total = lax.psum(jnp.sum(log_marg, axis=0), "docs")
    mean_log = grand_total / (docs_here * groups)
    mean_max = jnp.max(mean_log)
    mean_sum = jnp.sum(jnp.exp(mean_log - mean_max))
    new_log = mean_log - extent_supp(mean_max, mean_sum)
    return (row_pot, col_pot, new_log)


def solution(mesh):
    placed = (P("docs", None), P("supp", None), P("supp"), P("docs"), P("docs", None), P("docs"))
    return jax.shard_map(
        shards,
        mesh=mesh,
        in_specs=placed,
        out_specs=(P("docs", None), P("docs", "supp"), P("supp")),
        check_vma=False,
    )
```

profile of v0, /device:TPU:1, one launch (start us, length us, event | category | flops | bytes accessed | tf_op | source)
XLA Modules:
  0.0 547.9 jit_solution(805814266147628978)
XLA Ops:
  0.6 0.7 reduce.6
  1.4 4.5 reduce-window.6
  5.9 0.4 slice_reduce_fusion
  6.3 0.2 reduce-window.9
  6.5 0.1 add_add_fusion
  6.7 0.7 or_reduce_fusion
  7.4 0.7 multiply_reduce_fusion.2
  8.1 0.8 and_reduce_fusion
  8.9 6.0 %scatter_custom_fusion = s32[2048]{0:T(1024)} fusion(s32[1280]{0:T(1024)S(1)} %broadcast_select_fusion, s32[1280]{0:T(1024)} %param.11, s32[]{:T(128)} %constant.16.clone.1), kind=kCustom, calls=%fused_computation.55 | custom fusion | bytes 8704
  14.9 7.6 %all-to-all-start = ((s32[16,1,128]{2,1,0:T(1,128)}), s32[16,1,128]{2,1,0:T(1,128)S(1)}, u32[]{:S(2)}, u32[]{:S(2)}) async-start(s32[16,1,128]{2,1,0:T(1,128)} %bitcast.1), calls=%async_computation | async-start | bytes 16384 | tf_op jit(solution)/shard_map/all_to_all | solution.py:20
  22.5 7.1 %copy.11 = bf16[6250,300]{1,0:T(8,128)(2,1)} copy(bf16[6250,300]{0,1:T(8,128)(2,1)} %param.6) | data formatting | bytes 7500000 | tf_op args[0]
  29.6 10.3 %gather_fusion = bf16[2048,300]{1,0:T(8,128)(2,1)S(1)} fusion(bf16[6250,300]{1,0:T(8,128)(2,1)} %copy.11, s32[2048]{0:T(1024)S(1)} %fusion.8), kind=kCustom, calls=%fused_computation | custom fusion | bytes 2465792 | tf_op jit(solution)/shard_map/gather | solution.py:20
  39.9 1.6 copy.12
  41.5 6.7 %all-to-all-start.1 = ((bf16[16,128,300]{1,2,0:T(8,128)(2,1)}), bf16[16,128,300]{1,2,0:T(8,128)(2,1)}, u32[]{:S(2)}, u32[]{:S(2)}) async-start(bf16[16,128,300]{1,2,0:T(8,128)(2,1)} %copy.12), calls=%async_computation.1 | async-start | bytes 2490368 | tf_op jit(solution)/shard_map/all_to_all | solution.py:19
  48.2 0.6 reduce_max.67
  48.8 54.7 %pmax.28 = f32[]{:T(128)} all-reduce(f32[]{:T(128)} %reduce_max.67), channel_id=1, replica_groups=mesh['docs'=16,'supp'=32] {'supp'}, use_global_device_ids=true, to_apply=%region_1.2 | all-reduce | flops 1 | bytes 8 | tf_op jit(solution)/shard_map/pmax | solution.py:13
  104.9 1.3 exponential_reduce_fusion.3
  106.8 47.9 %psum.35 = f32[]{:T(128)} all-reduce(f32[]{:T(128)S(6)} %mul.57), channel_id=1, replica_groups=mesh['docs'=16,'supp'=32] {'supp'}, use_global_device_ids=true, to_apply=%region_3.4 | all-reduce | flops 1 | bytes 8 | tf_op jit(solution)/shard_map/psum | solution.py:14
  156.1 0.3 multiply_reduce_fusion
  156.4 0.1 iota_compare_fusion.2
  156.4 1.8 copy.13
  158.3 8.1 %gather_fusion.1 = bf16[1280,300]{1,0:T(8,128)(2,1)S(1)} fusion(bf16[16,128,300]{2,1,0:T(8,128)(2,1)S(1)} %copy.13, s32[1280]{0:T(1024)S(1)} %get-tuple-element.3), kind=kCustom, calls=%fused_computation.1 | custom fusion | bytes 1546240 | tf_op jit(solution)/shard_map/gather | solution.py:43
  166.4 6.8 %convolution_multiply_fusion = f32[1280,2048]{1,0:T(8,128)} fusion(bf16[1280,300]{1,0:T(8,128)(2,1)S(1)} %gather_fusion.1, bf16[2048,300]{0,1:T(8,128)(2,1)} %param.7), kind=kOutput, calls=%fused_computation.20 | convolution fusion | flops 1575485440 | bytes 12482560 | tf_op jit(solution)/shard_map/dot_general | solution.py:48
  173.2 0.3 multiply_reduce_fusion.1
  173.5 6.1 %select_reduce_fusion.5 = f32[2,2048]{1,0:T(2,128)S(1)} fusion(pred[2,640]{1,0:T(4,128)(4,1)S(1)} %iota_compare_fusion.2, f32[2,640,2048]{2,1,0:T(8,128)} %bitcast.41, f32[2048]{0:T(1024)S(1)} %multiply_reduce_fusion, f32[2,640]{1,0:T(2,128)S(1)} %add.104), kind=kLoop, calls=%fused_computation.17 | loop fusion | flops 15724544 | bytes 10516736 | tf_op jit(solution)/shard_map/reduce_max | solution.py:59
  179.6 0.9 copy-done
  180.5 4.1 select_reduce_fusion.4
  184.7 2.1 fusion.2
  186.7 3.0 exponential_reduce_fusion.1
  189.7 46.8 %pmax.29 = f32[2,640]{1,0:T(2,128)S(1)} all-reduce(f32[2,640]{1,0:T(2,128)S(1)} %reduce_max.70), channel_id=1, replica_groups=mesh['docs'=16,'supp'=32] {'supp'}, use_global_device_ids=true, to_apply=%region_13.14 | all-reduce | flops 1280 | bytes 10240 | tf_op jit(solution)/shard_map/pmax | solution.py:13
  236.5 47.0 %psum.36 = f32[2,640]{1,0:T(2,128)S(1)} all-reduce(f32[2,640]{1,0:T(2,128)S(1)} %exponential_multiply_fusion.1), channel_id=1, replica_groups=mesh['docs'=16,'supp'=32] {'supp'}, use_global_device_ids=true, to_apply=%region_15.16 | all-reduce | flops 1280 | bytes 10240 | tf_op jit(solution)/shard_map/psum | solution.py:14
  283.6 0.1 subtract_select_fusion.1
  283.6 6.7 %select_reduce_fusion.3 = f32[2,2048]{1,0:T(2,128)S(1)} fusion(f32[2,640]{1,0:T(2,128)S(1)} %subtract_select_fusion.1, pred[2,640]{1,0:T(4,128)(4,1)S(1)} %iota_compare_fusion.2, f32[2,640,2048]{2,1,0:T(8,128)} %bitcast.42, f32[2048]{0:T(1024)S(1)} %multiply_reduce_fusion, f32[2,640]{1,0:T(2,128)S(1)} %add.104), kind=kLoop, calls=%fused_computation.12 | loop fusion | flops 15724544 | bytes 10521856 | tf_op jit(solution)/shard_map/reduce_max | solution.py:59
  290.4 6.8 %select_reduce_fusion.2 = f32[2,2048]{1,0:T(2,128)S(1)} fusion(f32[2,2048]{1,0:T(2,128)S(1)} %select_reduce_fusion.3, f32[2,640]{1,0:T(2,128)S(1)} %subtract_select_fusion.1, pred[2,640]{1,0:T(4,128)(4,1)S(1)} %iota_compare_fusion.2, f32[2,640,2048]{2,1,0:T(8,128)} %bitcast.43, f32[2048]{0:T(1024)S(1)} %multiply_reduce_fusion, f32[2,640]{1,0:T(2,128)S(1)} %add.104), kind=kLoop, calls=%fused_computation.11 | loop fusion | flops 18345984 | bytes 10538240 | tf_op jit(solution)/shard_map/reduce_sum | solution.py:60
  297.2 0.0 copy-start.2
  297.2 2.1 fusion.3
  299.3 3.0 exponential_reduce_fusion
  302.3 46.8 %pmax.30 = f32[2,640]{1,0:T(2,128)S(1)} all-reduce(f32[2,640]{1,0:T(2,128)S(1)} %reduce_max.73), channel_id=1, replica_groups=mesh['docs'=16,'supp'=32] {'supp'}, use_global_device_ids=true, to_apply=%region_19.20 | all-reduce | flops 1280 | bytes 10240 | tf_op jit(solution)/shard_map/pmax | solution.py:13
  349.1 46.8 %psum.37 = f32[2,640]{1,0:T(2,128)S(1)} all-reduce(f32[2,640]{1,0:T(2,128)S(1)} %exponential_multiply_fusion), channel_id=1, replica_groups=mesh['docs'=16,'supp'=32] {'supp'}, use_global_device_ids=true, to_apply=%region_21.22 | all-reduce | flops 1280 | bytes 10240 | tf_op jit(solution)/shard_map/psum | solution.py:14
  395.9 0.1 subtract_select_fusion
  396.0 5.8 %select_reduce_fusion.1 = f32[2,2048]{1,0:T(2,128)S(1)} fusion(f32[2,640]{1,0:T(2,128)S(1)} %subtract_select_fusion, pred[2,640]{1,0:T(4,128)(4,1)S(1)} %iota_compare_fusion.2, f32[2,640,2048]{2,1,0:T(8,128)} %bitcast.44, f32[2048]{0:T(1024)S(1)} %multiply_reduce_fusion, f32[2,640]{1,0:T(2,128)S(1)} %add.104), kind=kLoop, calls=%fused_computation.8 | loop fusion | flops 15724544 | bytes 10521856 | tf_op jit(solution)/shard_map/reduce_max | solution.py:59
  401.7 6.6 %select_reduce_fusion = f32[2,2048]{1,0:T(2,128)S(1)} fusion(f32[2,2048]{1,0:T(2,128)S(1)} %select_reduce_fusion.1, f32[2,640]{1,0:T(2,128)S(1)} %subtract_select_fusion, pred[2,640]{1,0:T(4,128)(4,1)S(1)} %iota_compare_fusion.2, f32[2,640,2048]{2,1,0:T(8,128)} %bitcast.45, f32[2048]{0:T(1024)S(1)} %multiply_reduce_fusion, f32[2,640]{1,0:T(2,128)S(1)} %add.104), kind=kLoop, calls=%fused_computation.7 | loop fusion | flops 18345984 | bytes 10538240 | tf_op jit(solution)/shard_map/reduce_sum | solution.py:60
  408.4 33.7 %psum.38 = f32[2048]{0:T(1024)S(1)} all-reduce(f32[2048]{0:T(1024)S(1)} %add_reduce_fusion), channel_id=1, replica_groups=mesh['docs'=16,'supp'=32] {'docs'}, use_global_device_ids=true, to_apply=%region_25.26 | all-reduce | flops 2048 | bytes 16384 | tf_op jit(solution)/shard_map/psum | solution.py:77
  442.1 0.6 multiply_reduce_fusion.3
  442.7 53.8 %pmax.31 = f32[]{:T(128)} all-reduce(f32[]{:T(128)} %multiply_reduce_fusion.3), channel_id=1, replica_groups=mesh['docs'=16,'supp'=32] {'supp'}, use_global_device_ids=true, to_apply=%region_27.28 | all-reduce | flops 1 | bytes 8 | tf_op jit(solution)/shard_map/pmax | solution.py:13
  496.4 1.2 exponential_reduce_fusion.2
  499.6 46.3 %psum.39 = f32[]{:T(128)} all-reduce(f32[]{:T(128)S(6)} %mul.69), channel_id=1, replica_groups=mesh['docs'=16,'supp'=32] {'supp'}, use_global_device_ids=true, to_apply=%region_29.30 | all-reduce | flops 1 | bytes 8 | tf_op jit(solution)/shard_map/psum | solution.py:14
  547.3 0.6 multiply_subtract_fusion.2
  (35 shorter events, 0.3 us)
Async XLA Ops:
  14.9 14.7 %all-to-all-start = ((s32[16,1,128]{2,1,0:T(1,128)}), s32[16,1,128]{2,1,0:T(1,128)S(1)}, u32[]{:S(2)}, u32[]{:S(2)}) async-start(s32[16,1,128]{2,1,0:T(1,128)} %bitcast.1), calls=%async_computation | async-start | bytes 16384 | tf_op jit(solution)/shard_map/all_to_all | solution.py:20
  29.6 18.6 %copy-start.3 = (f32[2048]{0:T(1024)S(1)}, f32[2048]{0:T(1024)}, u32[]{:S(2)}) copy-start(f32[2048]{0:T(1024)} %param.8) | copy-start | bytes 24580
  29.6 126.4 %copy-start.1 = (bf16[2048,300]{0,1:T(8,128)(2,1)S(1)}, bf16[2048,300]{0,1:T(8,128)(2,1)}, u32[]{:S(2)}) copy-start(bf16[2048,300]{0,1:T(8,128)(2,1)} %param.7) | copy-start | bytes 3686404
  29.6 126.7 %copy-start.5 = (s32[2]{0:T(128)S(1)}, s32[2]{0:T(128)}, u32[]{:S(2)}) copy-start(s32[2]{0:T(128)} %param.9) | copy-start | bytes 28
  41.5 114.9 %all-to-all-start.1 = ((bf16[16,128,300]{1,2,0:T(8,128)(2,1)}), bf16[16,128,300]{1,2,0:T(8,128)(2,1)}, u32[]{:S(2)}, u32[]{:S(2)}) async-start(bf16[16,128,300]{1,2,0:T(8,128)(2,1)} %copy.12), calls=%async_computation.1 | async-start | bytes 2490368 | tf_op jit(solution)/shard_map/all_to_all | solution.py:19
  173.5 7.0 %copy-start = (f32[1280,2048]{1,0:T(8,128)S(1)}, f32[1280,2048]{1,0:T(8,128)}, u32[]{:S(2)}) copy-start(f32[1280,2048]{1,0:T(8,128)} %convolution_multiply_fusion) | copy-start | bytes 31457284
  283.6 13.5 %slice-start = ((s8[10485760]{0:T(1024)(128)(4,1)}), s8[4194304]{0:T(1024)(128)(4,1)S(1)}, s32[]{:S(2)}) async-start(s8[10485760]{0:T(1024)(128)(4,1)} %bitcast.47), calls=%async_computation.2 | async-start | bytes 8388608
  283.6 13.5 %slice-start.1 = ((s8[10485760]{0:T(1024)(128)(4,1)}), s8[4194304]{0:T(1024)(128)(4,1)S(1)}, s32[]{:S(2)}) async-start(s8[10485760]{0:T(1024)(128)(4,1)} %bitcast.47), calls=%async_computation.3 | async-start | bytes 8388608
  290.3 6.8 %slice-start.2 = ((s8[10485760]{0:T(1024)(128)(4,1)}), s8[2097152]{0:T(1024)(128)(4,1)S(1)}, s32[]{:S(2)}) async-start(s8[10485760]{0:T(1024)(128)(4,1)} %bitcast.47), calls=%async_computation.4 | async-start | bytes 4194304
  297.2 111.2 %copy-start.2 = (f32[2,2048]{1,0:T(2,128)}, f32[2,2048]{1,0:T(2,128)S(1)}, u32[]{:S(2)}) copy-start(f32[2,2048]{1,0:T(2,128)S(1)} %multiply_subtract_fusion) | copy-start | bytes 49156
  396.0 12.4 %copy-start.4 = (f32[2,640]{1,0:T(2,128)}, f32[2,640]{1,0:T(2,128)S(1)}, u32[]{:S(2)}) copy-start(f32[2,640]{1,0:T(2,128)S(1)} %subtract_select_fusion) | copy-start | bytes 15364
where the time goes:
time: 549 us; the launch traced here: 548 us
  blocking collectives  424 us (77%)
  other arithmetic  59.1 us (11%)
  local copies, waits for them, and re-layouts  36.3 us (7%)
  starting transfers between devices  14.3 us (3%)
  between operations  7.63 us (1%)
  matrix products  6.83 us (1%)
    pmax x4, blocking collectives, extent_supp(): global_max = lax.pmax(largest, 'supp')  202 us
    psum x4, blocking collectives, extent_supp(): global_sum = lax.psum(summed * jnp.exp(largest - global_max), 'supp')  188 us
    psum x1, blocking collectives, shards(): grand_total = lax.psum(jnp.sum(log_marg, axis=0), 'docs')  33.7 us
    reduce_max x3, other arithmetic, column_extent(): jnp.max(jnp.where(live_mask[:, :, None], scores, -jnp.inf), axis=1)  18.5 us
    reduce_sum x3, other arithmetic, column_extent(): jnp.sum(jnp.where(live_mask[:, :, None], jnp.exp(scores - largest[:, None...  17.5 us
    unnamed x20, local copies, waits for them, and re-layouts  14.1 us
    gather x2, local copies, waits for them, and re-layouts, fetch_rows(): vocab_table[lax.all_to_all(requests, 'docs', split_axis=0, concat_axis=0,...  11.9 us
  transfers between devices with their start and end apart: 2, of which 0 were waited for; matrix products, arithmetic and copies ran while one was open for 2% of the time, Pallas kernels for 0%

commit v1 on v0

v1 whole, which is shorter than its diff:
```python
import jax
import jax.numpy as jnp
from jax import lax
from jax.experimental import pallas as pl
from jax.experimental.pallas import tpu as pltpu
from jax.sharding import PartitionSpec as P

EPS = 0.05
LOG2E = 1.4426950408889634
LN2 = 0.6931471805599453
CAP = 128
HALF = CAP // 2
LANES = 128
FAR = 1e30
VMEM = pl.BlockSpec(memory_space=pltpu.VMEM)
SMEM = pl.BlockSpec(memory_space=pltpu.SMEM)
NT = (((1,), (1,)), ((), ()))


def call(kernel, out_shape, in_specs, scratch=(), limit=24):
    return pl.pallas_call(
        kernel,
        out_shape=out_shape,
        in_specs=in_specs,
        out_specs=jax.tree.map(lambda _: VMEM, out_shape),
        scratch_shapes=list(scratch),
        compiler_params=pltpu.CompilerParams(vmem_limit_bytes=limit << 20),
    )


def f32(shape):
    return jax.ShapeDtypeStruct(shape, jnp.float32)


def eye_mask():
    rows = lax.broadcasted_iota(jnp.int32, (LANES, LANES), 0)
    cols = lax.broadcasted_iota(jnp.int32, (LANES, LANES), 1)
    return rows == cols


def rowify(column, eye):
    return jnp.sum(jnp.where(eye, column, 0.0), axis=0, keepdims=True)


def colify(row, eye):
    return jnp.sum(jnp.where(eye, row, 0.0), axis=1, keepdims=True)


def request_kernel(core_ref, shard_ref, row_ref, req_ref, pos_ref):
    groups = req_ref.shape[0]
    slots = shard_ref.shape[1]
    core = core_ref[0]
    tri = (
        lax.broadcasted_iota(jnp.int32, (LANES, LANES), 0)
        <= lax.broadcasted_iota(jnp.int32, (LANES, LANES), 1)
    ).astype(jnp.bfloat16)
    owner_ids = lax.broadcasted_iota(jnp.int32, (groups, LANES), 0)
    seats = lax.broadcasted_iota(jnp.int32, (HALF, LANES), 0) + core * HALF
    seen = jnp.zeros((groups, 1), jnp.float32)
    req = jnp.zeros((2 * groups, HALF), jnp.float32)
    for block in range(slots // LANES):
        span = slice(block * LANES, (block + 1) * LANES)
        shard = shard_ref[:, span]
        row = row_ref[:, span]
        member = (owner_ids == shard).astype(jnp.float32)
        counted = seen + jnp.dot(member.astype(jnp.bfloat16), tri, preferred_element_type=jnp.float32)
        seen = counted[:, LANES - 1 :]
        rank = jnp.sum(member * (counted - 1.0), axis=0, keepdims=True).astype(jnp.int32)
        seated = (seats == rank).astype(jnp.float32).astype(jnp.bfloat16)
        high = member * (row >> 7).astype(jnp.float32)
        low = member * (row & 127).astype(jnp.float32)
        both = jnp.concatenate([high, low], axis=0).astype(jnp.bfloat16)
        req += lax.dot_general(both, seated, NT, preferred_element_type=jnp.float32)
        side = (rank >> 6) ^ core
        pos_ref[:, span] = side * (groups * HALF) + shard * HALF + (rank & (HALF - 1))
    req_ref[...] = (req[:groups] * 128.0 + req[groups:]).astype(jnp.int32)


def first_kernel(
    count_ref, own_ref, other_ref, pos_ref, atom_ref, logit_ref,
    plan_ref, sent_ref, peak_ref, start_ref,
    score_ref, head_ref, peak_col, mass_col,
):
    docs, atoms = start_ref.shape
    slots = plan_ref.shape[0]
    doc_slots = slots // docs
    half_rows = own_ref.shape[0]
    wide = min(512, atoms)
    for doc in range(docs):
        base = doc * doc_slots

        def score_step(step, top):
            at = pl.multiple_of(base + step * LANES, LANES)
            place = pos_ref[pl.ds(at, LANES), :]
            seats = lax.broadcasted_iota(jnp.int32, (LANES, half_rows), 1)
            own_hot = (seats == place).astype(jnp.float32).astype(jnp.bfloat16)
            other_hot = (seats + half_rows == place).astype(jnp.float32).astype(jnp.bfloat16)
            words = jnp.dot(own_hot, own_ref[...], preferred_element_type=jnp.float32)
            words += jnp.dot(other_hot, other_ref[...], preferred_element_type=jnp.float32)
            square = jnp.sum(words * words, axis=1, keepdims=True) * (LOG2E / EPS)
            slot = step * LANES + lax.broadcasted_iota(jnp.int32, (LANES, 1), 0)
            square = jnp.where(slot < count_ref[doc], square, FAR)
            words = words.astype(jnp.bfloat16)
            tops = []
            for left in range(0, atoms, wide):
                product = lax.dot_general(
                    words, atom_ref[left : left + wide, :], NT, preferred_element_type=jnp.float32
                )
                score = product * (2.0 * LOG2E / EPS) - square
                score_ref[pl.ds(at, LANES), left : left + wide] = score
                tops.append(jnp.max(score.reshape(LANES // 8, 8, wide), axis=0))
            return jnp.maximum(top, jnp.concatenate(tops, axis=1))

        top = lax.fori_loop(
            0, doc_slots // LANES, score_step, jnp.full((8, atoms), -jnp.inf, jnp.float32)
        )
        top = jnp.max(top, axis=0, keepdims=True)
        head_ref[...] = jnp.broadcast_to(top, (8, atoms))

        def sum_step(step, total):
            at = pl.multiple_of(base + step * 32, 32)
            for part in range(4):
                total += jnp.exp2(score_ref[pl.ds(at + part * 8, 8), :] - head_ref[...])
            return total

        total = lax.fori_loop(0, doc_slots // 32, sum_step, jnp.zeros((8, atoms), jnp.float32))
        total = jnp.sum(total, axis=0, keepdims=True)
        head = logit_ref[...] * LOG2E - top - jnp.log(total) * LOG2E
        start_ref[doc : doc + 1, :] = head
        head_ref[...] = jnp.broadcast_to(head, (8, atoms))

        def plan_step(step, carry):
            at = pl.multiple_of(base + step * 16, 16)
            upper = score_ref[pl.ds(at, 8), :] + head_ref[...]
            lower = score_ref[pl.ds(at + 8, 8), :] + head_ref[...]
            score = jnp.concatenate([upper, lower], axis=0)
            peak = jnp.max(score, axis=1, keepdims=True)
            share = jnp.exp2(score - peak)
            plan_ref[pl.ds(at, 16), :] = share.astype(plan_ref.dtype)
            peak_col[pl.ds(at, 16), :] = peak
            mass_col[pl.ds(at, 16), :] = jnp.sum(share, axis=1, keepdims=True)
            return carry

        lax.fori_loop(0, doc_slots // 16, plan_step, 0)

    eye = eye_mask()
    copies = sent_ref.shape[0]
    for block in range(slots // LANES):
        span = slice(block * LANES, (block + 1) * LANES)
        peak = rowify(peak_col[span, :], eye)
        mass = rowify(mass_col[span, :], eye)
        peak_ref[:, span] = peak
        extent = peak + jnp.log(mass) * LOG2E
        for copy in range(copies):
            sent_ref[copy, :, span] = extent
    logits = logit_ref[...] * LOG2E
    top = jnp.max(logits, axis=1, keepdims=True)
    whole = top + jnp.log(jnp.sum(jnp.exp2(logits - top), axis=1, keepdims=True)) * LOG2E
    for copy in range(copies):
        sent_ref[copy, :, slots:] = jnp.broadcast_to(whole, (1, LANES))


def slot_rows(count_ref, docs, slots):
    doc_slots = slots // docs
    lane = lax.broadcasted_iota(jnp.int32, (1, slots), 1)
    words = jnp.full((1, slots), count_ref[0], jnp.int32)
    first = jnp.zeros((1, slots), jnp.int32)
    for doc in range(1, docs):
        inside = lane >= doc * doc_slots
        words = jnp.where(inside, count_ref[doc], words)
        first = jnp.where(inside, doc * doc_slots, first)
    live = lane - first < words
    words = words.astype(jnp.float32)
    return live, words


def column_sums(plan_ref, weight_col, base, doc_slots):
    atoms = plan_ref.shape[1]

    def step_sum(step, total):
        at = pl.multiple_of(base + step * 16, 16)
        part = plan_ref[pl.ds(at, 16), :].astype(jnp.float32) * weight_col[pl.ds(at, 16), :]
        return total + part[:8] + part[8:]

    total = lax.fori_loop(0, doc_slots // 16, step_sum, jnp.zeros((8, atoms), jnp.float32))
    return jnp.sum(total, axis=0, keepdims=True)


def second_kernel(
    count_ref, got_ref, peak_ref, plan_ref, start_ref, logit_ref, square_ref,
    sent_ref, scale_ref, base_ref, gain_ref, col_ref,
    scale_col, mass_col, head_ref,
):
    docs, atoms = start_ref.shape
    slots = plan_ref.shape[0]
    doc_slots = slots // docs
    copies = got_ref.shape[0]
    top = got_ref[0]
    for copy in range(1, copies):
        top = jnp.maximum(top, got_ref[copy])
    mass = jnp.zeros_like(top)
    for copy in range(copies):
        mass += jnp.exp2(got_ref[copy] - top)
    extent = top + jnp.log(mass) * LOG2E
    whole = extent[:, slots : slots + 1]
    extent = extent[:, :slots]
    live, words = slot_rows(count_ref, docs, slots)
    scale = jnp.where(live, jnp.exp2(peak_ref[...] - extent) / words, 0.0)
    scale_ref[...] = scale
    base_ref[...] = (2.0 * EPS * LN2) * whole - EPS * jnp.log(words) - (EPS * LN2) * extent
    eye = eye_mask()
    for block in range(slots // LANES):
        span = slice(block * LANES, (block + 1) * LANES)
        scale_col[span, :] = colify(scale[:, span], eye)
    for doc in range(docs):
        base = doc * doc_slots
        total = column_sums(plan_ref, scale_col, base, doc_slots)
        gain_log = logit_ref[...] - jnp.log(total)
        gain = jnp.exp(gain_log)
        gain_ref[doc : doc + 1, :] = gain_log
        col_ref[doc : doc + 1, :] = (
            EPS * (LN2 * start_ref[doc : doc + 1, :] + gain_log)
            + square_ref[...]
            - (2.0 * EPS * LN2) * whole
        )
        head_ref[...] = jnp.broadcast_to(gain, (8, atoms))

        def row_step(step, carry):
            at = pl.multiple_of(base + step * 16, 16)
            part = plan_ref[pl.ds(at, 16), :].astype(jnp.float32)
            upper = jnp.sum(part[:8] * head_ref[...], axis=1, keepdims=True)
            lower = jnp.sum(part[8:] * head_ref[...], axis=1, keepdims=True)
            mass_col[pl.ds(at, 8), :] = upper
            mass_col[pl.ds(at + 8, 8), :] = lower
            return carry

        lax.fori_loop(0, doc_slots // 16, row_step, 0)
    for block in range(slots // LANES):
        span = slice(block * LANES, (block + 1) * LANES)
        part = rowify(mass_col[span, :], eye) * scale[:, span]
        for copy in range(copies):
            sent_ref[copy, :, span] = part


def third_kernel(
    count_ref, got_ref, scale_ref, base_ref, plan_ref, gain_ref,
    sent_ref, row_ref,
    scale_col,
):
    docs, atoms = gain_ref.shape
    slots = plan_ref.shape[0]
    doc_slots = slots // docs
    mass = got_ref[0]
    for copy in range(1, got_ref.shape[0]):
        mass += got_ref[copy]
    live, words = slot_rows(count_ref, docs, slots)
    mass = jnp.where(live, mass, 1.0) * words
    row_ref[...] = jnp.where(live, base_ref[...] - EPS * jnp.log(mass), 0.0)
    scale = scale_ref[...] / mass
    eye = eye_mask()
    for block in range(slots // LANES):
        span = slice(block * LANES, (block + 1) * LANES)
        scale_col[span, :] = colify(scale[:, span], eye)
    marginal = jnp.zeros((1, atoms), jnp.float32)
    for doc in range(docs):
        total = column_sums(plan_ref, scale_col, doc * doc_slots, doc_slots)
        marginal += gain_ref[doc : doc + 1, :] + jnp.log(total)
    for copy in range(sent_ref.shape[0]):
        sent_ref[copy] = marginal


def mean_kernel(documents, got_ref, mean_ref, sent_ref):
    total = got_ref[0]
    for copy in range(1, got_ref.shape[0]):
        total += got_ref[copy]
    mean = total * (1.0 / documents)
    mean_ref[...] = mean
    top = jnp.max(mean, axis=1, keepdims=True)
    extent = top + jnp.log(jnp.sum(jnp.exp(mean - top), axis=1, keepdims=True))
    for copy in range(sent_ref.shape[0]):
        sent_ref[copy] = jnp.broadcast_to(extent, (1, LANES))


def final_kernel(got_ref, mean_ref, new_ref):
    top = got_ref[0]
    for copy in range(1, got_ref.shape[0]):
        top = jnp.maximum(top, got_ref[copy])
    mass = jnp.zeros_like(top)
    for copy in range(got_ref.shape[0]):
        mass += jnp.exp(got_ref[copy] - top)
    extent = top + jnp.log(mass)
    new_ref[...] = mean_ref[...] - extent[:, :1]


def swap(x, axis):
    return lax.all_to_all(x, axis, split_axis=0, concat_axis=0, tiled=True)


def shards(vocab_table, support_atoms, weight_logits, word_counts, word_shard, word_row):
    groups = lax.axis_size("docs")
    parts = lax.axis_size("supp")
    docs = word_counts.shape[0]
    slots = word_row.shape[0]
    atoms, width = support_atoms.shape
    core = (lax.axis_index("supp") & 1).astype(jnp.int32).reshape(1)

    requests, place = call(
        request_kernel,
        (
            jax.ShapeDtypeStruct((groups, HALF), jnp.int32),
            jax.ShapeDtypeStruct((1, slots), jnp.int32),
        ),
        [SMEM, VMEM, VMEM],
        limit=8,
    )(core, word_shard.reshape(1, slots), word_row.reshape(1, slots))
    asked = swap(requests.reshape(groups, 1, HALF), "docs")
    found = vocab_table[asked.reshape(groups * HALF)]
    own = swap(found.reshape(groups, HALF, width), "docs").reshape(groups * HALF, width)
    other = lax.ppermute(own, "supp", [(i, i ^ 1) for i in range(parts)])

    logits = weight_logits.reshape(1, atoms)
    square = jnp.sum(jnp.square(support_atoms.astype(jnp.float32)), axis=1).reshape(1, atoms)
    plan, extent, peak, start = call(
        first_kernel,
        (
            jax.ShapeDtypeStruct((slots, atoms), jnp.bfloat16),
            f32((parts, 1, slots + LANES)),
            f32((1, slots)),
            f32((docs, atoms)),
        ),
        [SMEM, VMEM, VMEM, VMEM, VMEM, VMEM],
        [
            pltpu.VMEM((slots, atoms), jnp.float32),
            pltpu.VMEM((8, atoms), jnp.float32),
            pltpu.VMEM((slots, 1), jnp.float32),
            pltpu.VMEM((slots, 1), jnp.float32),
        ],
        limit=40,
    )(word_counts, own, other, place.reshape(slots, 1), support_atoms, logits)
    extents = swap(extent, "supp")
    mass, scale, base, gain, col_pot = call(
        second_kernel,
        (
            f32((parts, 1, slots)),
            f32((1, slots)),
            f32((1, slots)),
            f32((docs, atoms)),
            f32((docs, atoms)),
        ),
        [SMEM, VMEM, VMEM, VMEM, VMEM, VMEM, VMEM],
        [
            pltpu.VMEM((slots, 1), jnp.float32),
            pltpu.VMEM((slots, 1), jnp.float32),
            pltpu.VMEM((8, atoms), jnp.float32),
        ],
    )(word_counts, extents, peak, plan, start, logits, square)
    masses = swap(mass, "supp")
    marginal, row_pot = call(
        third_kernel,
        (f32((groups, 1, atoms)), f32((1, slots))),
        [SMEM, VMEM, VMEM, VMEM, VMEM, VMEM],
        [pltpu.VMEM((slots, 1), jnp.float32)],
    )(word_counts, masses, scale, base, plan, gain)
    marginals = swap(marginal, "docs")
    mean, part = call(
        lambda *refs: mean_kernel(docs * groups, *refs),
        (f32((1, atoms)), f32((parts, 1, LANES))),
        [VMEM],
    )(marginals)
    new_log = call(final_kernel, f32((1, atoms)), [VMEM, VMEM])(swap(part, "supp"), mean)
    return row_pot.reshape(docs, slots // docs), col_pot, new_log.reshape(atoms)


def solution(mesh):
    placed = (P("docs", None), P("supp", None), P("supp"), P("docs"), P("docs", None), P("docs"))
    return jax.shard_map(
        shards,
        mesh=mesh,
        in_specs=placed,
        out_specs=(P("docs", None), P("docs", "supp"), P("supp")),
        check_vma=False,
    )
```

time: 549 us -> 199 us (0.36)
  blocking collectives: 424 us -> 48.7 us
  other arithmetic: 59.1 us -> 2.27 us
  Pallas kernels: 0 us -> 55.9 us
  waiting for transfers between devices: 0.01 us -> 27.6 us
  starting transfers between devices: 14.3 us -> 35.5 us
  local copies, waits for them, and re-layouts: 36.3 us -> 27 us
  between operations: 7.63 us -> 0.78 us
  matrix products: 6.83 us -> 0 us
    psum x5 -> x0, blocking collectives: 222 us -> none  [the longest x4 188 us: extent_supp(): global_sum = lax.psum(summed * jnp.exp(largest - global_max), 'supp')]
    pmax x4 -> x0, blocking collectives: 202 us -> none  [extent_supp(): global_max = lax.pmax(largest, 'supp')]
    pallas_call x0 -> x6, Pallas kernels: none -> 55.9 us  [the longest x1 29.6 us: shards(): call(first_kernel, (jax.ShapeDtypeStruct((slots, atoms), jnp.bfloat16), f...]
    all_to_all x0 -> x3, blocking collectives: none -> 48.7 us  [swap(): return lax.all_to_all(x, axis, split_axis=0, concat_axis=0, tiled=True)]
    all_to_all x2 -> x3, waiting for transfers between devices: 0.01 us -> 27.6 us  [swap(): return lax.all_to_all(x, axis, split_axis=0, concat_axis=0, tiled=True)]
    reduce_sum x11 -> x1, other arithmetic: 26.5 us -> 1.57 us  [shards(): jnp.sum(jnp.square(support_atoms.astype(jnp.float32)), axis=1)]
    reduce_max x7 -> x0, other arithmetic: 23.9 us -> none  [the longest x3 18.5 us: column_extent(): jnp.max(jnp.where(live_mask[:, :, None], scores, -jnp.inf), axis=1)]
    all_to_all x2 -> x3, starting transfers between devices: 14.3 us -> 29.5 us  [swap(): return lax.all_to_all(x, axis, split_axis=0, concat_axis=0, tiled=True)]
  transfers between devices with their start and end apart: 2 -> 4, of which waited for: 0 -> 2; matrix products, arithmetic and copies ran while one was open for 2% -> 6% of each run, Pallas kernels for 0% -> 0%
where the time goes in v1:
time: 199 us; the launch traced here: 198 us
  Pallas kernels  55.9 us (28%)
  blocking collectives  48.7 us (24%)
  starting transfers between devices  35.5 us (18%)
  waiting for transfers between devices  27.6 us (14%)
  local copies, waits for them, and re-layouts  27 us (14%)
  other arithmetic  2.27 us (1%)
    all_to_all x3, blocking collectives, swap(): return lax.all_to_all(x, axis, split_axis=0, concat_axis=0, tiled=True)  48.7 us
    pallas_call x1, Pallas kernels, shards(): call(first_kernel, (jax.ShapeDtypeStruct((slots, atoms), jnp.bfloat16), f...  29.6 us
    all_to_all x3, starting transfers between devices, swap(): return lax.all_to_all(x, axis, split_axis=0, concat_axis=0, tiled=True)  29.5 us
    all_to_all x3, waiting for transfers between devices, swap(): return lax.all_to_all(x, axis, split_axis=0, concat_axis=0, tiled=True)  27.6 us
    pallas_call x1, Pallas kernels, shards(): call(second_kernel, (f32((parts, 1, slots)), f32((1, slots)), f32((1, slo...  15.9 us
    unnamed x16, local copies, waits for them, and re-layouts  15.5 us
    pallas_call x1, Pallas kernels, shards(): call(third_kernel, (f32((groups, 1, atoms)), f32((1, slots))), [SMEM, VME...  7.41 us
    gather x1, local copies, waits for them, and re-layouts, shards(): found = vocab_table[asked.reshape(groups * HALF)]  6.75 us
  transfers between devices with their start and end apart: 4, of which 2 were waited for; matrix products, arithmetic and copies ran while one was open for 6% of the time, Pallas kernels for 0%

profile of v1, /device:TPU:1, one launch (start us, length us, event | category | flops | bytes accessed | tf_op | source)
XLA Modules:
  0.0 197.7 jit_solution(7664906954834157456)
XLA Ops:
  0.6 0.7 reshape.72.row_ref
  1.3 0.0 copy-start.5
  1.3 0.7 copy-done.5
  2.0 1.5 shard_map.85
  3.5 7.6 %all-to-all-start = ((s32[16,1,64]{2,1,0:T(1,128)}), s32[16,1,64]{2,1,0:T(1,128)S(1)}, u32[]{:S(2)}, u32[]{:S(2)}) async-start(s32[16,1,64]{2,1,0:T(1,128)} %bitcast.3), calls=%async_computation | async-start | bytes 16384 | tf_op jit(solution)/shard_map/all_to_all | solution.py:296
  11.1 7.1 %copy.15 = bf16[6250,300]{1,0:T(8,128)(2,1)} copy(bf16[6250,300]{0,1:T(8,128)(2,1)} %param.6) | data formatting | bytes 7500000 | tf_op args[0]
  18.2 0.0 all-to-all-done
  18.2 0.5 broadcast.22
  18.7 0.7 reduce.4
  19.4 0.1 reshape.74
  19.5 6.8 %gather_fusion = bf16[1024,300]{1,0:T(8,128)(2,1)S(1)} fusion(bf16[6250,300]{1,0:T(8,128)(2,1)} %copy.15, s32[1024]{0:T(1024)S(1)} %broadcast_clamp_fusion), kind=kCustom, calls=%fused_computation | custom fusion | bytes 1232896 | tf_op jit(solution)/shard_map/gather | solution.py:317
  26.3 17.7 %all_to_all.30 = bf16[16,64,300]{2,1,0:T(8,128)(2,1)S(1)} all-to-all(bf16[16,64,300]{2,1,0:T(8,128)(2,1)S(1)} %bitcast.19), channel_id=1, replica_groups=mesh['docs'=16,'supp'=32] {'docs'}, dimensions={0} | all-to-all | bytes 1228800 | tf_op jit(solution)/shard_map/all_to_all | solution.py:296
  43.9 0.3 copy.16
  44.2 0.0 copy-start.4
  44.2 0.0 copy-start.6
  44.3 6.0 %collective-permute-start = (bf16[1024,300]{0,1:T(8,128)(2,1)S(1)}, bf16[1024,300]{0,1:T(8,128)(2,1)}, u32[]{:S(2)}, u32[]{:S(2)}) collective-permute-start(bf16[1024,300]{0,1:T(8,128)(2,1)S(1)} %copy.16), channel_id=1, source_target_pairs={{0,1},{1,0},{2,3},{3,2},{4,5},{5,4},{6,7},{7,6},{8,9},{9,8},{10,11... | collective-permute-start | bytes 1843208 | tf_op jit(solution)/shard_map/ppermute | solution.py:319
  50.3 1.1 copy.18.pos_ref
  51.4 1.8 copy.19.atom_ref
  53.2 0.0 collective-permute-done
  53.2 1.4 copy.17.other_ref
  54.6 0.0 copy-done.4
  54.6 0.0 copy-done.6
  54.7 0.0 copy-start.3
  54.7 1.1 copy-done.3
  55.7 29.6 %shard_map.86 = (bf16[1280,2048]{1,0:T(8,128)(2,1)S(1)}, f32[32,1,1408]{2,1,0:T(1,128)}, f32[1,1280]{1,0:T(1,128)S(1)}, f32[2,2048]{1,0:T(2,128)S(1)}) custom-call(s32[2]{0:T(128)S(1)} %copy-done.6, bf16[1024,300]{1,0:T(8,128)(2,1)S(1)} %bitcast.13, bf16[1024,300]{1,0:T(8,128)(2,1)S(1)} %copy.17.other_ref, s32[1280,1]{1,0:T(8,128)S(1)} %copy-done.3, ...), custom_call_target="tpu_custom_call" | custom-call | tf_op jit(solution)/shard_map/pallas_call | solution.py:323
  85.3 0.0 copy-start
  85.3 2.3 %copy-done = bf16[1280,2048]{1,0:T(8,128)(2,1)} copy-done((bf16[1280,2048]{1,0:T(8,128)(2,1)}, bf16[1280,2048]{1,0:T(8,128)(2,1)S(1)}, u32[]{:S(2)}) %copy-start) | copy-done | bytes 5242904
  87.6 15.4 %all-to-all-start.2 = ((f32[32,1,1408]{2,1,0:T(1,128)}), f32[32,1,1408]{2,1,0:T(1,128)S(1)}, u32[]{:S(2)}, u32[]{:S(2)}) async-start(f32[32,1,1408]{2,1,0:T(1,128)} %get-tuple-element.20), calls=%async_computation.2 | async-start | bytes 360448 | tf_op jit(solution)/shard_map/all_to_all | solution.py:296
  103.0 1.6 multiply_reduce_fusion
  104.6 16.3 %all-to-all-done.2.got_ref = f32[32,1,1408]{2,1,0:T(1,128)S(1)} async-done(((f32[32,1,1408]{2,1,0:T(1,128)}), f32[32,1,1408]{2,1,0:T(1,128)S(1)}, u32[]{:S(2)}, u32[]{:S(2)}) %all-to-all-start.2) | async-done | bytes 180256 | tf_op jit(solution)/shard_map/all_to_all | solution.py:296
  120.8 0.0 copy-start.1
  120.8 2.5 %copy-done.1 = bf16[1280,2048]{1,0:T(8,128)(2,1)S(1)} copy-done((bf16[1280,2048]{1,0:T(8,128)(2,1)S(1)}, bf16[1280,2048]{1,0:T(8,128)(2,1)}, u32[]{:S(2)}) %copy-start.1) | copy-done | bytes 5242904
  123.3 0.0 copy-start.2
  123.3 15.9 %shard_map.87 = (f32[32,1,1280]{2,1,0:T(1,128)S(1)}, f32[1,1280]{1,0:T(1,128)S(1)}, f32[1,1280]{1,0:T(1,128)S(1)}, f32[2,2048]{1,0:T(2,128)S(1)}, f32[2,2048]{1,0:T(2,128)}) custom-call(s32[2]{0:T(128)S(1)} %copy-done.6, f32[32,1,1408]{2,1,0:T(1,128)S(1)} %all-to-all-done.2.got_ref, f32[1,1280]{1,0:T(1,128)S(1)} %get-tuple-element.21.peak_ref, ...), custom_call_target="tpu_custom_call" | custom-call | tf_op jit(solution)/shard_map/pallas_call | solution.py:341
  139.2 21.5 %all_to_all.31.got_ref = f32[32,1,1280]{2,1,0:T(1,128)S(1)} all-to-all(f32[32,1,1280]{2,1,0:T(1,128)S(1)} %get-tuple-element.24), channel_id=1, replica_groups=mesh['docs'=16,'supp'=32] {'supp'}, dimensions={0} | all-to-all | bytes 327680 | tf_op jit(solution)/shard_map/all_to_all | solution.py:296
  160.7 0.0 copy-done.2
  160.7 7.4 %shard_map.88 = (f32[16,1,2048]{2,1,0:T(1,128)S(1)}, f32[1,1280]{1,0:T(1,128)S(1)}) custom-call(s32[2]{0:T(128)S(1)} %copy-done.6, f32[32,1,1280]{2,1,0:T(1,128)S(1)} %all_to_all.31.got_ref, f32[1,1280]{1,0:T(1,128)S(1)} %get-tuple-element.25.scale_ref, f32[1,1280]{1,0:T(1,128)S(1)} %get-tuple-element.26.base_ref, bf16[1280,2048]{1,0:T(8,128)(2,1)S(1)} %copy-done.2, ...), custom_call_target="tpu_custom_call" | custom-call | tf_op jit(solution)/shard_map/pallas_call | solution.py:358
  168.1 9.5 %all_to_all.32.refs_0_ = f32[16,1,2048]{2,1,0:T(1,128)S(1)} all-to-all(f32[16,1,2048]{2,1,0:T(1,128)S(1)} %get-tuple-element.30), channel_id=1, replica_groups=mesh['docs'=16,'supp'=32] {'docs'}, dimensions={0} | all-to-all | bytes 262144 | tf_op jit(solution)/shard_map/all_to_all | solution.py:296
  177.6 0.8 shard_map.89
  178.5 6.6 %all-to-all-start.5 = ((f32[32,1,128]{2,1,0:T(1,128)}), f32[32,1,128]{2,1,0:T(1,128)S(1)}, u32[]{:S(2)}, u32[]{:S(2)}) async-start(f32[32,1,128]{2,1,0:T(1,128)} %get-tuple-element.31), calls=%async_computation.5 | async-start | bytes 32768 | tf_op jit(solution)/shard_map/all_to_all | solution.py:296
  185.0 0.6 reshape.80
  185.6 11.3 %all-to-all-done.5.got_ref = f32[32,1,128]{2,1,0:T(1,128)S(1)} async-done(((f32[32,1,128]{2,1,0:T(1,128)}), f32[32,1,128]{2,1,0:T(1,128)S(1)}, u32[]{:S(2)}, u32[]{:S(2)}) %all-to-all-start.5) | async-done | bytes 16416 | tf_op jit(solution)/shard_map/all_to_all | solution.py:296
  197.0 0.8 shard_map.90
  (3 shorter events, 0.0 us)
Async XLA Ops:
  1.3 0.7 copy-start.5
  3.5 14.7 %all-to-all-start = ((s32[16,1,64]{2,1,0:T(1,128)}), s32[16,1,64]{2,1,0:T(1,128)S(1)}, u32[]{:S(2)}, u32[]{:S(2)}) async-start(s32[16,1,64]{2,1,0:T(1,128)} %bitcast.3), calls=%async_computation | async-start | bytes 16384 | tf_op jit(solution)/shard_map/all_to_all | solution.py:296
  44.2 10.4 %copy-start.4 = (f32[2048]{0:T(1024)S(1)}, f32[2048]{0:T(1024)}, u32[]{:S(2)}) copy-start(f32[2048]{0:T(1024)} %param.8) | copy-start | bytes 24580
  44.2 10.4 %copy-start.6 = (s32[2]{0:T(128)S(1)}, s32[2]{0:T(128)}, u32[]{:S(2)}) copy-start(s32[2]{0:T(128)} %count_ref.5) | copy-start | bytes 28
  44.3 8.9 %collective-permute-start = (bf16[1024,300]{0,1:T(8,128)(2,1)S(1)}, bf16[1024,300]{0,1:T(8,128)(2,1)}, u32[]{:S(2)}, u32[]{:S(2)}) collective-permute-start(bf16[1024,300]{0,1:T(8,128)(2,1)S(1)} %copy.16), channel_id=1, source_target_pairs={{0,1},{1,0},{2,3},{3,2},{4,5},{5,4},{6,7},{7,6},{8,9},{9,8},{10,11... | collective-permute-start | bytes 1843208 | tf_op jit(solution)/shard_map/ppermute | solution.py:319
  54.7 1.1 copy-start.3
  85.3 2.3 %copy-start = (bf16[1280,2048]{1,0:T(8,128)(2,1)}, bf16[1280,2048]{1,0:T(8,128)(2,1)S(1)}, u32[]{:S(2)}) copy-start(bf16[1280,2048]{1,0:T(8,128)(2,1)S(1)} %get-tuple-element.22.plan_ref) | copy-start | bytes 15728644
  87.6 33.2 %all-to-all-start.2 = ((f32[32,1,1408]{2,1,0:T(1,128)}), f32[32,1,1408]{2,1,0:T(1,128)S(1)}, u32[]{:S(2)}, u32[]{:S(2)}) async-start(f32[32,1,1408]{2,1,0:T(1,128)} %get-tuple-element.20), calls=%async_computation.2 | async-start | bytes 360448 | tf_op jit(solution)/shard_map/all_to_all | solution.py:296
  120.8 2.5 %copy-start.1 = (bf16[1280,2048]{1,0:T(8,128)(2,1)S(1)}, bf16[1280,2048]{1,0:T(8,128)(2,1)}, u32[]{:S(2)}) copy-start(bf16[1280,2048]{1,0:T(8,128)(2,1)} %copy-done) | copy-start | bytes 15728644
  123.3 37.4 %copy-start.2 = (bf16[1280,2048]{1,0:T(8,128)(2,1)S(1)}, bf16[1280,2048]{1,0:T(8,128)(2,1)}, u32[]{:S(2)}) copy-start(bf16[1280,2048]{1,0:T(8,128)(2,1)} %copy-done) | copy-start | bytes 15728644
  178.5 18.5 %all-to-all-start.5 = ((f32[32,1,128]{2,1,0:T(1,128)}), f32[32,1,128]{2,1,0:T(1,128)S(1)}, u32[]{:S(2)}, u32[]{:S(2)}) async-start(f32[32,1,128]{2,1,0:T(1,128)} %get-tuple-element.31), calls=%async_computation.5 | async-start | bytes 32768 | tf_op jit(solution)/shard_map/all_to_all | solution.py:296

commit v2 on v1

v2 whole, which is shorter than its diff:
```python
import jax
import jax.numpy as jnp
from jax import lax
from jax.experimental import pallas as pl
from jax.experimental.pallas import tpu as pltpu
from jax.sharding import PartitionSpec as P

EPS = 0.05
LOG2E = 1.4426950408889634
LN2 = 0.6931471805599453
CAP = 128
HALF = CAP // 2
LANES = 128
FAR = 1e30
WIDE = 256
VMEM = pl.BlockSpec(memory_space=pltpu.VMEM)
SMEM = pl.BlockSpec(memory_space=pltpu.SMEM)
NT = (((1,), (1,)), ((), ()))


def call(kernel, out_shape, in_specs, scratch=(), limit=24):
    return pl.pallas_call(
        kernel,
        out_shape=out_shape,
        in_specs=in_specs,
        out_specs=jax.tree.map(lambda _: VMEM, out_shape),
        scratch_shapes=list(scratch),
        compiler_params=pltpu.CompilerParams(vmem_limit_bytes=limit << 20),
    )


def f32(shape):
    return jax.ShapeDtypeStruct(shape, jnp.float32)


def eye_mask():
    rows = lax.broadcasted_iota(jnp.int32, (LANES, LANES), 0)
    cols = lax.broadcasted_iota(jnp.int32, (LANES, LANES), 1)
    return rows == cols


def rowify(column, eye):
    return jnp.sum(jnp.where(eye, column, 0.0), axis=0, keepdims=True)


def colify(row, eye):
    return jnp.sum(jnp.where(eye, row, 0.0), axis=1, keepdims=True)


def request_kernel(core_ref, shard_ref, row_ref, req_ref, pos_ref):
    groups = req_ref.shape[0]
    slots = shard_ref.shape[1]
    doc_slots = pos_ref.shape[1]
    core = core_ref[0]
    tri = (
        lax.broadcasted_iota(jnp.int32, (LANES, LANES), 0)
        <= lax.broadcasted_iota(jnp.int32, (LANES, LANES), 1)
    ).astype(jnp.bfloat16)
    owner_ids = lax.broadcasted_iota(jnp.int32, (groups, LANES), 0)
    seats = lax.broadcasted_iota(jnp.int32, (HALF, LANES), 0) + core * HALF
    seen = jnp.zeros((groups, 1), jnp.float32)
    req = jnp.zeros((2 * groups, HALF), jnp.float32)
    places = []
    for block in range(slots // LANES):
        span = slice(block * LANES, (block + 1) * LANES)
        shard = shard_ref[:, span]
        row = row_ref[:, span]
        member = (owner_ids == shard).astype(jnp.float32)
        counted = seen + jnp.dot(member.astype(jnp.bfloat16), tri, preferred_element_type=jnp.float32)
        seen = counted[:, LANES - 1 :]
        rank = jnp.sum(member * (counted - 1.0), axis=0, keepdims=True).astype(jnp.int32)
        seated = (seats == rank).astype(jnp.float32).astype(jnp.bfloat16)
        high = member * (row >> 7).astype(jnp.float32)
        low = member * (row & 127).astype(jnp.float32)
        both = jnp.concatenate([high, low], axis=0).astype(jnp.bfloat16)
        req += lax.dot_general(both, seated, NT, preferred_element_type=jnp.float32)
        side = (rank >> 6) ^ core
        places.append(side * (groups * HALF) + shard * HALF + (rank & (HALF - 1)))
    req_ref[...] = (req[:groups] * 128.0 + req[groups:]).astype(jnp.int32)
    own_blocks = doc_slots // LANES
    for block in range(own_blocks):
        span = slice(block * LANES, (block + 1) * LANES)
        pos_ref[:, span] = jnp.where(core == 0, places[block], places[own_blocks + block])


def own_count(core_ref, count_ref):
    return jnp.where(core_ref[0] == 0, count_ref[0], count_ref[1])


def first_kernel(
    core_ref, count_ref, own_ref, other_ref, pos_ref,
    own_atom_ref, other_atom_ref, own_logit_ref, other_logit_ref,
    plan_ref, sent_ref, peak_ref, start_ref,
    hot_ref, word_ref, square_ref, score_refs, far_refs, head_ref, near_ref, mass_ref,
):
    slots, all_atoms = plan_ref.shape
    half_rows = own_ref.shape[0]
    quarters = len(score_refs)
    quarter = all_atoms // quarters
    blocks = slots // LANES
    count = own_count(core_ref, count_ref)
    eye = eye_mask()
    seats = lax.broadcasted_iota(jnp.int32, (LANES, 2 * half_rows), 1).astype(jnp.float32)
    for block in range(blocks):
        span = slice(block * LANES, (block + 1) * LANES)
        place = colify(pos_ref[:, span].astype(jnp.float32), eye)
        hot_ref[span, :] = (seats == place).astype(jnp.float32).astype(jnp.bfloat16)
    words = jnp.dot(hot_ref[:, :half_rows], own_ref[...], preferred_element_type=jnp.float32)
    words += jnp.dot(hot_ref[:, half_rows:], other_ref[...], preferred_element_type=jnp.float32)
    square = jnp.sum(words * words, axis=1, keepdims=True) * (LOG2E / EPS)
    slot = lax.broadcasted_iota(jnp.int32, (slots, 1), 0)
    square = jnp.where(slot < count, square, FAR)
    square_ref[...] = jnp.broadcast_to(square, (slots, LANES))
    word_ref[...] = words.astype(jnp.bfloat16)
    for far_ref in far_refs:
        far_ref[...] = jnp.full(far_ref.shape, -jnp.inf, jnp.float32)

    def score_step(step, carry):
        at = pl.multiple_of(step * WIDE, WIDE)
        for part in range(quarters):
            half, inner = divmod(part, quarters // 2)
            atom_ref = (own_atom_ref, other_atom_ref)[half]
            logit_ref = (own_logit_ref, other_logit_ref)[half]
            score_ref, far_ref = score_refs[part], far_refs[part]
            source = pl.ds(pl.multiple_of(inner * quarter + at, WIDE), WIDE)
            product = jnp.dot(word_ref[...], atom_ref[:, source], preferred_element_type=jnp.float32)
            tiles = [
                product[:, left : left + LANES] * (2.0 * LOG2E / EPS) - square_ref[...]
                for left in range(0, WIDE, LANES)
            ]
            for tile, score in enumerate(tiles):
                score_ref[:, pl.ds(at + tile * LANES, LANES)] = score
            score = score_ref[:, pl.ds(at, WIDE)]
            top = jnp.max(score, axis=0, keepdims=True)
            total = jnp.sum(jnp.exp2(score - top), axis=0, keepdims=True)
            head = logit_ref[:, source] * LOG2E - top - jnp.log(total) * LOG2E
            start_ref[:, pl.ds(pl.multiple_of(part * quarter + at, WIDE), WIDE)] = head
            far = far_ref[...]
            for left in range(0, WIDE, LANES):
                far = jnp.maximum(
                    far, score_ref[:, pl.ds(at + left, LANES)] + head[:, left : left + LANES]
                )
            far_ref[...] = far
        return carry

    lax.fori_loop(0, quarter // WIDE, score_step, 0)
    head_ref[...] = jnp.broadcast_to(start_ref[...], (8, all_atoms))
    for block in range(blocks):
        span = slice(block * LANES, (block + 1) * LANES)
        far = far_refs[0][span, :]
        for far_ref in far_refs[1:]:
            far = jnp.maximum(far, far_ref[span, :])
        peak = jnp.max(far, axis=1, keepdims=True)
        near_ref[span, :] = jnp.broadcast_to(peak, (LANES, LANES))
        peak_ref[:, span] = rowify(peak, eye)

    def plan_step(step, carry):
        for group in range(2):
            at = pl.multiple_of(step * 32 + group * 16, 16)
            masses = [jnp.zeros((8, LANES), jnp.float32) for _ in range(2)]
            near = [near_ref[pl.ds(at + 8 * side, 8), :] for side in range(2)]
            for left in range(0, all_atoms, LANES):
                part, inner = divmod(left, quarter)
                shares = []
                for side in range(2):
                    score = score_refs[part][pl.ds(at + 8 * side, 8), inner : inner + LANES]
                    share = jnp.exp2(score + head_ref[:, left : left + LANES] - near[side])
                    masses[side] += share
                    shares.append(share)
                plan_ref[pl.ds(at, 16), left : left + LANES] = jnp.concatenate(
                    shares, axis=0
                ).astype(plan_ref.dtype)
            for side in range(2):
                mass_ref[pl.ds(at + 8 * side, 8), :] = masses[side]
        return carry

    lax.fori_loop(0, slots // 32, plan_step, 0)
    copies = sent_ref.shape[0]
    for block in range(blocks):
        span = slice(block * LANES, (block + 1) * LANES)
        mass = jnp.sum(mass_ref[span, :], axis=1, keepdims=True)
        extent = peak_ref[:, span] + jnp.log(rowify(mass, eye)) * LOG2E
        for copy in range(copies):
            sent_ref[copy, :, span] = extent
    own_logits = own_logit_ref[...] * LOG2E
    other_logits = other_logit_ref[...] * LOG2E
    top = jnp.max(jnp.maximum(own_logits, other_logits), axis=1, keepdims=True)
    whole = jnp.sum(jnp.exp2(own_logits - top) + jnp.exp2(other_logits - top), axis=1, keepdims=True)
    whole = top + jnp.log(whole) * LOG2E
    for copy in range(copies):
        sent_ref[copy, :, slots:] = jnp.broadcast_to(whole, (1, LANES))


def pieces(row):
    high = row.astype(jnp.bfloat16).astype(jnp.float32)
    line = lax.broadcasted_iota(jnp.int32, (8, row.shape[1]), 0)
    return jnp.where(line == 0, high, jnp.where(line == 1, row - high, 0.0)).astype(jnp.bfloat16)


def column_sums(weights, plan_ref, left, wide):
    sums = jnp.dot(weights, plan_ref[:, left : left + wide], preferred_element_type=jnp.float32)
    return jnp.sum(sums, axis=0, keepdims=True)


def second_kernel(
    core_ref, count_ref, got_ref, peak_ref, plan_ref, start_ref, own_logit_ref, other_logit_ref,
    sent_ref, scale_ref, base_ref, gain_ref, own_col_ref, other_col_ref,
):
    slots, all_atoms = plan_ref.shape
    atoms = all_atoms // 2
    copies = got_ref.shape[0]
    top = got_ref[0]
    for copy in range(1, copies):
        top = jnp.maximum(top, got_ref[copy])
    mass = jnp.zeros_like(top)
    for copy in range(copies):
        mass += jnp.exp2(got_ref[copy] - top)
    extent = top + jnp.log(mass) * LOG2E
    whole = extent[:, slots : slots + 1]
    extent = extent[:, :slots]
    count = own_count(core_ref, count_ref)
    live = lax.broadcasted_iota(jnp.int32, (1, slots), 1) < count
    words = jnp.full((1, slots), count, jnp.int32).astype(jnp.float32)
    scale = jnp.where(live, jnp.exp2(peak_ref[...] - extent) / words, 0.0)
    scale_ref[...] = scale
    base_ref[...] = (2.0 * EPS * LN2) * whole - EPS * jnp.log(words) - (EPS * LN2) * extent
    weights = pieces(scale)
    part = jnp.zeros((8, slots), jnp.float32)
    wide = min(512, atoms)
    for left in range(0, all_atoms, wide):
        half, inner = divmod(left, atoms)
        logit_ref = (own_logit_ref, other_logit_ref)[half]
        col_ref = (own_col_ref, other_col_ref)[half]
        total = column_sums(weights, plan_ref, left, wide)
        gain_log = logit_ref[:, inner : inner + wide] - jnp.log(total)
        gain_ref[:, left : left + wide] = gain_log
        col_ref[:, inner : inner + wide] = EPS * (
            LN2 * start_ref[:, left : left + wide] + gain_log
        ) - (2.0 * EPS * LN2) * whole
        part += lax.dot_general(
            pieces(jnp.exp(gain_log)), plan_ref[:, left : left + wide], NT,
            preferred_element_type=jnp.float32,
        )
    part = jnp.sum(part, axis=0, keepdims=True) * scale
    for copy in range(copies):
        sent_ref[copy] = part


def third_kernel(
    core_ref, count_ref, got_ref, scale_ref, base_ref, plan_ref, gain_ref, other_col_ref,
    sent_ref, pass_ref,
):
    slots, all_atoms = plan_ref.shape
    atoms = all_atoms // 2
    mass = got_ref[0]
    for copy in range(1, got_ref.shape[0]):
        mass += got_ref[copy]
    core = core_ref[0]
    count = own_count(core_ref, count_ref)
    live = lax.broadcasted_iota(jnp.int32, (1, slots), 1) < count
    words = jnp.full((1, slots), count, jnp.int32).astype(jnp.float32)
    mass = jnp.where(live, mass, 1.0) * words
    pass_ref[:, :slots] = jnp.where(live, base_ref[...] - EPS * jnp.log(mass), 0.0)
    pass_ref[:, slots:] = other_col_ref[...]
    weights = pieces(scale_ref[...] / mass)
    wide = min(512, atoms)
    for left in range(0, all_atoms, wide):
        half, inner = divmod(left, atoms)
        total = column_sums(weights, plan_ref, left, wide)
        marginal = gain_ref[:, left : left + wide] + jnp.log(total)
        place = core if half == 0 else 1 - core
        for group in range(sent_ref.shape[0] // 2):
            sent_ref[2 * group + place, :, inner : inner + wide] = marginal


def mean_kernel(documents, got_ref, mean_ref, sent_ref):
    total = got_ref[0]
    for copy in range(1, got_ref.shape[0]):
        total += got_ref[copy]
    mean = total * (1.0 / documents)
    mean_ref[...] = mean
    top = jnp.max(mean, axis=1, keepdims=True)
    extent = top + jnp.log(jnp.sum(jnp.exp(mean - top), axis=1, keepdims=True))
    for copy in range(sent_ref.shape[0]):
        sent_ref[copy] = jnp.broadcast_to(extent, (1, LANES))


def final_kernel(got_ref, mean_ref, new_ref):
    top = got_ref[0]
    for copy in range(1, got_ref.shape[0]):
        top = jnp.maximum(top, got_ref[copy])
    mass = jnp.zeros_like(top)
    for copy in range(got_ref.shape[0]):
        mass += jnp.exp(got_ref[copy] - top)
    extent = top + jnp.log(mass)
    new_ref[...] = mean_ref[...] - extent[:, :1]


def output_kernel(core_ref, pass_ref, back_ref, own_col_ref, atom_ref, row_ref, col_ref):
    slots = row_ref.shape[1]
    atom = atom_ref[...].astype(jnp.float32)
    square = jnp.sum(atom * atom, axis=0, keepdims=True)
    core = core_ref[0]
    own, other = pass_ref[:, :slots], back_ref[:, :slots]
    own_col, other_col = own_col_ref[...] + square, back_ref[:, slots:] + square
    row_ref[0:1, :] = jnp.where(core == 0, own, other)
    row_ref[1:2, :] = jnp.where(core == 0, other, own)
    col_ref[0:1, :] = jnp.where(core == 0, own_col, other_col)
    col_ref[1:2, :] = jnp.where(core == 0, other_col, own_col)


def swap(x, axis, lists=None):
    return lax.all_to_all(
        x, axis, split_axis=0, concat_axis=0, tiled=True, axis_index_groups=lists
    )


def shards(vocab_table, support_atoms, weight_logits, word_counts, word_shard, word_row):
    groups = lax.axis_size("docs")
    parts = lax.axis_size("supp")
    docs = word_counts.shape[0]
    slots = word_row.shape[0]
    doc_slots = slots // docs
    atoms, width = support_atoms.shape
    core = (lax.axis_index("supp") & 1).astype(jnp.int32).reshape(1)
    pairs = [(i, i ^ 1) for i in range(parts)]
    same_core = [list(range(side, parts, 2)) for side in range(2)]
    same_level = [
        [doc * parts + level + side for doc in range(groups) for side in range(2)]
        for level in range(0, parts, 2)
    ]

    requests, place = call(
        request_kernel,
        (
            jax.ShapeDtypeStruct((groups, HALF), jnp.int32),
            jax.ShapeDtypeStruct((1, doc_slots), jnp.int32),
        ),
        [SMEM, VMEM, VMEM],
        limit=8,
    )(core, word_shard.reshape(1, slots), word_row.reshape(1, slots))
    asked = swap(requests.reshape(groups, 1, HALF), "docs")
    own_atoms = support_atoms.T
    other_atoms = lax.ppermute(own_atoms, "supp", pairs)
    own_logits = weight_logits.reshape(1, atoms)
    other_logits = lax.ppermute(own_logits, "supp", pairs)
    found = vocab_table[asked.reshape(groups * HALF)]
    own = swap(found.reshape(groups, HALF, width), "docs").reshape(groups * HALF, width)
    other = lax.ppermute(own, "supp", pairs)

    quarters = 4
    quarter = 2 * atoms // quarters
    plan, extent, peak, start = call(
        first_kernel,
        (
            jax.ShapeDtypeStruct((doc_slots, 2 * atoms), jnp.bfloat16),
            f32((parts // 2, 1, doc_slots + LANES)),
            f32((1, doc_slots)),
            f32((1, 2 * atoms)),
        ),
        [SMEM, SMEM] + [VMEM] * 7,
        [
            pltpu.VMEM((doc_slots, 2 * groups * HALF), jnp.bfloat16),
            pltpu.VMEM((doc_slots, width), jnp.bfloat16),
            pltpu.VMEM((doc_slots, LANES), jnp.float32),
            [pltpu.VMEM((doc_slots, quarter), jnp.float32)] * quarters,
            [pltpu.VMEM((doc_slots, LANES), jnp.float32)] * quarters,
            pltpu.VMEM((8, 2 * atoms), jnp.float32),
            pltpu.VMEM((doc_slots, LANES), jnp.float32),
            pltpu.VMEM((doc_slots, LANES), jnp.float32),
        ],
        limit=32,
    )(core, word_counts, own, other, place, own_atoms, other_atoms, own_logits, other_logits)
    extents = swap(extent, "supp", same_core)
    mass, scale, base, gain, own_col, other_col = call(
        second_kernel,
        (
            f32((parts // 2, 1, doc_slots)),
            f32((1, doc_slots)),
            f32((1, doc_slots)),
            f32((1, 2 * atoms)),
            f32((1, atoms)),
            f32((1, atoms)),
        ),
        [SMEM, SMEM] + [VMEM] * 6,
        limit=12,
    )(core, word_counts, extents, peak, plan, start, own_logits, other_logits)
    masses = swap(mass, "supp", same_core)
    marginal, passed = call(
        third_kernel,
        (f32((2 * groups, 1, atoms)), f32((1, doc_slots + atoms))),
        [SMEM, SMEM] + [VMEM] * 6,
        limit=12,
    )(core, word_counts, masses, scale, base, plan, gain, other_col)
    marginals = swap(marginal, ("docs", "supp"), same_level)
    back = lax.ppermute(passed, "supp", pairs)
    mean, part = call(
        lambda *refs: mean_kernel(docs * groups, *refs),
        (f32((1, atoms)), f32((parts, 1, LANES))),
        [VMEM],
        limit=8,
    )(marginals)
    shares = swap(part, "supp")
    row_pot, col_pot = call(
        output_kernel,
        (f32((docs, doc_slots)), f32((docs, atoms))),
        [SMEM] + [VMEM] * 4,
        limit=8,
    )(core, passed, back, own_col, own_atoms)
    new_log = call(final_kernel, f32((1, atoms)), [VMEM, VMEM], limit=8)(shares, mean)
    return row_pot, col_pot, new_log.reshape(atoms)


def solution(mesh):
    placed = (P("docs", None), P("supp", None), P("supp"), P("docs"), P("docs", None), P("docs"))
    return jax.shard_map(
        shards,
        mesh=mesh,
        in_specs=placed,
        out_specs=(P("docs", None), P("docs", "supp"), P("supp")),
        check_vma=False,
    )
```

time: 199 us -> 148 us (0.74)
  Pallas kernels: 55.9 us -> 22.4 us
  blocking collectives: 48.7 us -> 74.2 us
  waiting for transfers between devices: 27.6 us -> 9.73 us
  starting transfers between devices: 35.5 us -> 23.1 us
  local copies, waits for them, and re-layouts: 27 us -> 16.6 us
    pallas_call x4 -> x5, Pallas kernels: 53.6 us -> 20 us  [the longest x1 13.6 us: shards(): call(first_kernel, (jax.ShapeDtypeStruct((doc_slots, 2 * atoms), jnp.bflo...]
    all_to_all x3 -> x4, blocking collectives: 48.7 us -> 74.2 us  [swap(): lax.all_to_all(x, axis, split_axis=0, concat_axis=0, tiled=True, axis_ind...]
    all_to_all x3 -> x2, waiting for transfers between devices: 27.6 us -> 8.14 us  [swap(): lax.all_to_all(x, axis, split_axis=0, concat_axis=0, tiled=True, axis_ind...]
    all_to_all x3 -> x2, starting transfers between devices: 29.5 us -> 11.2 us  [swap(): lax.all_to_all(x, axis, split_axis=0, concat_axis=0, tiled=True, axis_ind...]
    unnamed x16 -> x9, local copies, waits for them, and re-layouts: 15.5 us -> 7.82 us
    ppermute x1 -> x4, starting transfers between devices: 5.99 us -> 11.9 us  [the longest x1 4.65 us: shards(): other_atoms = lax.ppermute(own_atoms, 'supp', pairs)]
  transfers between devices with their start and end apart: 4 -> 6, of which waited for: 2 -> 3; matrix products, arithmetic and copies ran while one was open for 6% -> 11% of each run, Pallas kernels for 0% -> 0%
where the time goes in v2:
time: 148 us; the launch traced here: 147 us
  blocking collectives  74.2 us (50%)
  starting transfers between devices  23.1 us (16%)
  Pallas kernels  22.4 us (15%)
  local copies, waits for them, and re-layouts  16.6 us (11%)
  waiting for transfers between devices  9.73 us (7%)
    all_to_all x4, blocking collectives, swap(): lax.all_to_all(x, axis, split_axis=0, concat_axis=0, tiled=True, axis_ind...  74.2 us
    pallas_call x1, Pallas kernels, shards(): call(first_kernel, (jax.ShapeDtypeStruct((doc_slots, 2 * atoms), jnp.bflo...  13.6 us
    all_to_all x2, starting transfers between devices, swap(): lax.all_to_all(x, axis, split_axis=0, concat_axis=0, tiled=True, axis_ind...  11.2 us
    all_to_all x2, waiting for transfers between devices, swap(): lax.all_to_all(x, axis, split_axis=0, concat_axis=0, tiled=True, axis_ind...  8.14 us
    unnamed x9, local copies, waits for them, and re-layouts  7.82 us
    gather x1, local copies, waits for them, and re-layouts, shards(): found = vocab_table[asked.reshape(groups * HALF)]  6.85 us
    ppermute x1, starting transfers between devices, shards(): other_atoms = lax.ppermute(own_atoms, 'supp', pairs)  4.65 us
    pallas_call x1, Pallas kernels, shards(): call(second_kernel, (f32((parts // 2, 1, doc_slots)), f32((1, doc_slots))...  3.6 us
  transfers between devices with their start and end apart: 6, of which 3 were waited for; matrix products, arithmetic and copies ran while one was open for 11% of the time, Pallas kernels for 0%

profile of v2, /device:TPU:1, one launch (start us, length us, event | category | flops | bytes accessed | tf_op | source)
XLA Modules:
  0.0 147.4 jit_solution(9209969831620907134)
XLA Ops:
  0.6 0.7 reshape.63.row_ref
  1.3 0.0 copy-start.2
  1.3 0.7 copy-done.2
  2.0 1.5 %shard_map.85 = (s32[16,64]{1,0:T(8,128)}, s32[1,640]{1,0:T(1,128)S(1)}) custom-call(s32[1]{0:T(128)} %bitcast.core_ref, s32[1,1280]{1,0:T(1,128)S(1)} %bitcast.19, s32[1,1280]{1,0:T(1,128)S(1)} %reshape.63.row_ref), custom_call_target="tpu_custom_call" | custom-call | tf_op jit(solution)/shard_map/pallas_call | solution.py:333
  3.5 7.6 %all-to-all-start = ((s32[16,1,64]{2,1,0:T(1,128)}), s32[16,1,64]{2,1,0:T(1,128)S(1)}, u32[]{:S(2)}, u32[]{:S(2)}) async-start(s32[16,1,64]{2,1,0:T(1,128)} %bitcast.3), calls=%async_computation | async-start | bytes 16384 | tf_op jit(solution)/shard_map/all_to_all | solution.py:313
  11.1 4.6 %collective-permute-start.1 = (bf16[300,2048]{1,0:T(8,128)(2,1)}, bf16[300,2048]{1,0:T(8,128)(2,1)}, u32[]{:S(2)}, u32[]{:S(2)}) collective-permute-start(bf16[300,2048]{1,0:T(8,128)(2,1)} %bitcast.13), channel_id=1, source_target_pairs={{0,1},{1,0},{2,3},{3,2},{4,5},{5,4},{6,7},{7,6},{8,9},{9,8},{10,11... | collective-permute-start | bytes 3686408 | tf_op jit(solution)/shard_map/ppermute | solution.py:344
  15.8 7.1 %copy.11 = bf16[6250,300]{1,0:T(8,128)(2,1)} copy(bf16[6250,300]{0,1:T(8,128)(2,1)} %param.6) | data formatting | bytes 7500000 | tf_op args[0]
  22.9 0.0 all-to-all-done
  22.9 0.5 broadcast.21
  23.4 0.7 reduce.3
  24.1 0.1 reshape.65
  24.2 0.0 copy-start.1
  24.2 0.0 copy-start
  24.2 0.0 copy-start.3
  24.2 6.9 %gather_fusion = bf16[1024,300]{1,0:T(8,128)(2,1)S(1)} fusion(bf16[6250,300]{1,0:T(8,128)(2,1)} %copy.11, s32[1024]{0:T(1024)S(1)} %broadcast_clamp_fusion), kind=kCustom, calls=%fused_computation | custom fusion | bytes 1232896 | tf_op jit(solution)/shard_map/gather | solution.py:347
  31.1 20.8 %all_to_all.30 = bf16[16,64,300]{2,1,0:T(8,128)(2,1)S(1)} all-to-all(bf16[16,64,300]{2,1,0:T(8,128)(2,1)S(1)} %bitcast.20), channel_id=1, replica_groups=mesh['docs'=16,'supp'=32] {'docs'}, dimensions={0} | all-to-all | bytes 1228800 | tf_op jit(solution)/shard_map/all_to_all | solution.py:313
  51.9 0.3 copy.12
  52.2 3.1 %collective-permute-start = (bf16[1024,300]{0,1:T(8,128)(2,1)S(1)}, bf16[1024,300]{0,1:T(8,128)(2,1)S(1)}, u32[]{:S(2)}, u32[]{:S(2)}) collective-permute-start(bf16[1024,300]{0,1:T(8,128)(2,1)S(1)} %copy.12), channel_id=1, source_target_pairs={{0,1},{1,0},{2,3},{3,2},{4,5},{5,4},{6,7},{7,6},{8,9},{9,8},{10,11... | collective-permute-start | bytes 1843208 | tf_op jit(solution)/shard_map/ppermute | solution.py:349
  55.2 0.0 copy-done.1
  55.2 1.9 %collective-permute-start.2 = (f32[1,2048]{1,0:T(1,128)S(1)}, f32[1,2048]{1,0:T(1,128)S(1)}, u32[]{:S(2)}, u32[]{:S(2)}) collective-permute-start(f32[1,2048]{1,0:T(1,128)S(1)} %bitcast.16), channel_id=1, source_target_pairs={{0,1},{1,0},{2,3},{3,2},{4,5},{5,4},{6,7},{7,6},{8,9},{9,8},{10,11... | collective-permute-start | bytes 24584 | tf_op jit(solution)/shard_map/ppermute | solution.py:346
  57.2 0.0 collective-permute-done
  57.2 0.4 copy.13.other_ref
  57.5 0.8 collective-permute-done.2.other_logit_ref
  58.3 0.0 collective-permute-done.1.other_atom_ref
  58.3 0.0 copy-done
  58.3 0.0 copy-done.3
  58.3 13.6 %shard_map.86 = (bf16[640,4096]{1,0:T(8,128)(2,1)S(1)}, f32[16,1,768]{2,1,0:T(1,128)S(1)}, f32[1,640]{1,0:T(1,128)S(1)}, f32[1,4096]{1,0:T(1,128)S(1)}) custom-call(s32[1]{0:T(128)} %bitcast.core_ref, s32[2]{0:T(128)S(1)} %copy-done.3, bf16[1024,300]{1,0:T(8,128)(2,1)S(1)} %bitcast.12, bf16[1024,300]{1,0:T(8,128)(2,1)S(1)} %copy.13.other_ref, ...), custom_call_target="tpu_custom_call" | custom-call | tf_op jit(solution)/shard_map/pallas_call | solution.py:353
  71.9 24.6 %all_to_all.31.got_ref = f32[16,1,768]{2,1,0:T(1,128)S(1)} all-to-all(f32[16,1,768]{2,1,0:T(1,128)S(1)} %get-tuple-element.23), channel_id=1, replica_groups={{0,2,4,6,8,10,12,14,16,18,20,22,24,26,28,30},{1,3,5,7,9,11,13,15,17,19,..., dimensions={0} | all-to-all | bytes 98304 | tf_op jit(solution)/shard_map/all_to_all | solution.py:313
  96.6 3.6 %shard_map.87 = (f32[16,1,640]{2,1,0:T(1,128)S(1)}, f32[1,640]{1,0:T(1,128)S(1)}, f32[1,640]{1,0:T(1,128)S(1)}, f32[1,4096]{1,0:T(1,128)S(1)}, f32[1,2048]{1,0:T(1,128)S(1)}, /*index=5*/f32[1,2048]{1,0:T(1,128)S(1)}) custom-call(s32[1]{0:T(128)} %bitcast.core_ref, s32[2]{0:T(128)S(1)} %copy-done.3, f32[16,1,768]{2,1,0:T(1,128)S(1)} %all_to_all.31.got_ref, ...), custom_call_target="tpu_custom_call" | custom-call | tf_op jit(solution)/shard_map/pallas_call | solution.py:375
  100.2 14.6 %all_to_all.32.got_ref = f32[16,1,640]{2,1,0:T(1,128)S(1)} all-to-all(f32[16,1,640]{2,1,0:T(1,128)S(1)} %get-tuple-element.27), channel_id=1, replica_groups={{0,2,4,6,8,10,12,14,16,18,20,22,24,26,28,30},{1,3,5,7,9,11,13,15,17,19,..., dimensions={0} | all-to-all | bytes 81920 | tf_op jit(solution)/shard_map/all_to_all | solution.py:313
  114.8 1.4 shard_map.88
  116.2 14.1 %all_to_all.33.refs_0_ = f32[32,1,2048]{2,1,0:T(1,128)S(1)} all-to-all(f32[32,1,2048]{2,1,0:T(1,128)S(1)} %get-tuple-element.36), channel_id=1, replica_groups={{0,1,32,33,64,65,96,97,128,129,160,161,192,193,224,225,256,257,288,289,..., dimensions={0} | all-to-all | bytes 524288 | tf_op jit(solution)/shard_map/all_to_all | solution.py:313
  130.3 0.8 shard_map.90
  131.1 3.6 %all-to-all-start.5 = ((f32[32,1,128]{2,1,0:T(1,128)}), f32[32,1,128]{2,1,0:T(1,128)S(1)}, u32[]{:S(2)}, u32[]{:S(2)}) async-start(f32[32,1,128]{2,1,0:T(1,128)} %get-tuple-element.37), calls=%async_computation.5 | async-start | bytes 32768 | tf_op jit(solution)/shard_map/all_to_all | solution.py:313
  134.7 2.3 %collective-permute-start.3 = (f32[1,2688]{1,0:T(1,128)S(1)}, f32[1,2688]{1,0:T(1,128)S(1)}, u32[]{:S(2)}, u32[]{:S(2)}) collective-permute-start(f32[1,2688]{1,0:T(1,128)S(1)} %get-tuple-element.32.pass_ref), channel_id=1, source_target_pairs={{0,1},{1,0},{2,3},{3,2},{4,5},{5,4},{6,7},{7,6},{8,9},{9,8},{10,11... | collective-permute-start | bytes 32264 | tf_op jit(solution)/shard_map/ppermute | solution.py:396
  137.0 0.8 collective-permute-done.3.back_ref
  137.8 0.7 shard_map.89
  138.5 8.1 %all-to-all-done.5.got_ref = f32[32,1,128]{2,1,0:T(1,128)S(1)} async-done(((f32[32,1,128]{2,1,0:T(1,128)}), f32[32,1,128]{2,1,0:T(1,128)S(1)}, u32[]{:S(2)}, u32[]{:S(2)}) %all-to-all-start.5) | async-done | bytes 16416 | tf_op jit(solution)/shard_map/all_to_all | solution.py:313
  146.7 0.8 shard_map.91
  (2 shorter events, 0.0 us)
Async XLA Ops:
  1.3 0.7 copy-start.2
  3.5 19.4 %all-to-all-start = ((s32[16,1,64]{2,1,0:T(1,128)}), s32[16,1,64]{2,1,0:T(1,128)S(1)}, u32[]{:S(2)}, u32[]{:S(2)}) async-start(s32[16,1,64]{2,1,0:T(1,128)} %bitcast.3), calls=%async_computation | async-start | bytes 16384 | tf_op jit(solution)/shard_map/all_to_all | solution.py:313
  11.1 47.2 %collective-permute-start.1 = (bf16[300,2048]{1,0:T(8,128)(2,1)}, bf16[300,2048]{1,0:T(8,128)(2,1)}, u32[]{:S(2)}, u32[]{:S(2)}) collective-permute-start(bf16[300,2048]{1,0:T(8,128)(2,1)} %bitcast.13), channel_id=1, source_target_pairs={{0,1},{1,0},{2,3},{3,2},{4,5},{5,4},{6,7},{7,6},{8,9},{9,8},{10,11... | collective-permute-start | bytes 3686408 | tf_op jit(solution)/shard_map/ppermute | solution.py:344
  24.2 31.0 %copy-start.1 = (f32[2048]{0:T(1024)S(1)}, f32[2048]{0:T(1024)}, u32[]{:S(2)}) copy-start(f32[2048]{0:T(1024)} %param.8) | copy-start | bytes 24580
  24.2 34.1 %copy-start = (bf16[2048,300]{0,1:T(8,128)(2,1)S(1)}, bf16[2048,300]{0,1:T(8,128)(2,1)}, u32[]{:S(2)}) copy-start(bf16[2048,300]{0,1:T(8,128)(2,1)} %param.7) | copy-start | bytes 3686404
  24.2 34.1 %copy-start.3 = (s32[2]{0:T(128)S(1)}, s32[2]{0:T(128)}, u32[]{:S(2)}) copy-start(s32[2]{0:T(128)} %count_ref.5) | copy-start | bytes 28
  52.2 5.0 %collective-permute-start = (bf16[1024,300]{0,1:T(8,128)(2,1)S(1)}, bf16[1024,300]{0,1:T(8,128)(2,1)S(1)}, u32[]{:S(2)}, u32[]{:S(2)}) collective-permute-start(bf16[1024,300]{0,1:T(8,128)(2,1)S(1)} %copy.12), channel_id=1, source_target_pairs={{0,1},{1,0},{2,3},{3,2},{4,5},{5,4},{6,7},{7,6},{8,9},{9,8},{10,11... | collective-permute-start | bytes 1843208 | tf_op jit(solution)/shard_map/ppermute | solution.py:349
  55.2 3.1 %collective-permute-start.2 = (f32[1,2048]{1,0:T(1,128)S(1)}, f32[1,2048]{1,0:T(1,128)S(1)}, u32[]{:S(2)}, u32[]{:S(2)}) collective-permute-start(f32[1,2048]{1,0:T(1,128)S(1)} %bitcast.16), channel_id=1, source_target_pairs={{0,1},{1,0},{2,3},{3,2},{4,5},{5,4},{6,7},{7,6},{8,9},{9,8},{10,11... | collective-permute-start | bytes 24584 | tf_op jit(solution)/shard_map/ppermute | solution.py:346
  131.1 15.6 %all-to-all-start.5 = ((f32[32,1,128]{2,1,0:T(1,128)}), f32[32,1,128]{2,1,0:T(1,128)S(1)}, u32[]{:S(2)}, u32[]{:S(2)}) async-start(f32[32,1,128]{2,1,0:T(1,128)} %get-tuple-element.37), calls=%async_computation.5 | async-start | bytes 32768 | tf_op jit(solution)/shard_map/all_to_all | solution.py:313
  134.7 3.1 %collective-permute-start.3 = (f32[1,2688]{1,0:T(1,128)S(1)}, f32[1,2688]{1,0:T(1,128)S(1)}, u32[]{:S(2)}, u32[]{:S(2)}) collective-permute-start(f32[1,2688]{1,0:T(1,128)S(1)} %get-tuple-element.32.pass_ref), channel_id=1, source_target_pairs={{0,1},{1,0},{2,3},{3,2},{4,5},{5,4},{6,7},{7,6},{8,9},{9,8},{10,11... | collective-permute-start | bytes 32264 | tf_op jit(solution)/shard_map/ppermute | solution.py:396

commit v3 on v2

--- a/solution.py
+++ b/solution.py
@@ -4,6 +4,7 @@
 from jax.experimental import pallas as pl
 from jax.experimental.pallas import tpu as pltpu
 from jax.sharding import PartitionSpec as P
+
 
 EPS = 0.05
 LOG2E = 1.4426950408889634
@@ -13,6 +14,7 @@
 LANES = 128
 FAR = 1e30
 WIDE = 256
+TILES = 3
 VMEM = pl.BlockSpec(memory_space=pltpu.VMEM)
 SMEM = pl.BlockSpec(memory_space=pltpu.SMEM)
 NT = (((1,), (1,)), ((), ()))
@@ -64,7 +66,7 @@
     for block in range(slots // LANES):
         span = slice(block * LANES, (block + 1) * LANES)
         shard = shard_ref[:, span]
-        row = row_ref[:, span]
+        row = row_ref[span].reshape(1, LANES)
         member = (owner_ids == shard).astype(jnp.float32)
         counted = seen + jnp.dot(member.astype(jnp.bfloat16), tri, preferred_element_type=jnp.float32)
         seen = counted[:, LANES - 1 :]
@@ -83,6 +85,44 @@
         pos_ref[:, span] = jnp.where(core == 0, places[block], places[own_blocks + block])
 
 
+def lookup_kernel(asked_ref, vocab_ref, found_ref, table_ref, line_ref):
+    width, rows = vocab_ref.shape
+    groups = asked_ref.shape[0]
+    seats = asked_ref.shape[2]
+    count = found_ref.shape[0]
+    sides = lax.broadcasted_iota(jnp.int32, (WIDE, WIDE), 0)
+    same = (sides == lax.broadcasted_iota(jnp.int32, (WIDE, WIDE), 1)).astype(jnp.float32)
+    same = same.astype(jnp.bfloat16)
+    tiles = [(tile, min(LANES, width - tile * LANES)) for tile in range(TILES)]
+
+    def spread(first, some):
+        turned = lax.dot_general(
+            same[:some, :some], vocab_ref[:, pl.ds(first, some)], NT,
+            preferred_element_type=jnp.float32,
+        )
+        for tile, lanes in tiles:
+            left = tile * LANES
+            table_ref[pl.ds(first * TILES + tile, some, stride=TILES), :lanes] = turned[
+                :, left : left + lanes
+            ]
+
+    for first in range(0, rows, WIDE):
+        spread(first, min(WIDE, rows - first))
+
+    def line_step(group, carry):
+        first = pl.multiple_of(group * (seats * TILES), 8)
+        for seat in range(seats):
+            row = asked_ref[group, 0, seat]
+            line_ref[pl.ds(first + seat * TILES, 8), :] = table_ref[pl.ds(row * TILES, 8), :]
+        return carry
+
+    lax.fori_loop(0, groups, line_step, 0)
+    for tile, lanes in tiles:
+        found_ref[:, tile * LANES : (tile + 1) * LANES] = line_ref[
+            pl.ds(tile, count, stride=TILES), :
+        ].astype(found_ref.dtype)
+
+
 def own_count(core_ref, count_ref):
     return jnp.where(core_ref[0] == 0, count_ref[0], count_ref[1])
 
@@ -91,12 +131,10 @@
     core_ref, count_ref, own_ref, other_ref, pos_ref,
     own_atom_ref, other_atom_ref, own_logit_ref, other_logit_ref,
     plan_ref, sent_ref, peak_ref, start_ref,
-    hot_ref, word_ref, square_ref, score_refs, far_refs, head_ref, near_ref, mass_ref,
+    hot_ref, word_ref, square_ref, score_ref, far_ref, head_ref, near_ref, mass_ref,
 ):
     slots, all_atoms = plan_ref.shape
     half_rows = own_ref.shape[0]
-    quarters = len(score_refs)
-    quarter = all_atoms // quarters
     blocks = slots // LANES
     count = own_count(core_ref, count_ref)
     eye = eye_mask()
@@ -107,63 +145,78 @@
         hot_ref[span, :] = (seats == place).astype(jnp.float32).astype(jnp.bfloat16)
     words = jnp.dot(hot_ref[:, :half_rows], own_ref[...], preferred_element_type=jnp.float32)
     words += jnp.dot(hot_ref[:, half_rows:], other_ref[...], preferred_element_type=jnp.float32)
+    words = words[:, : word_ref.shape[1]]
     square = jnp.sum(words * words, axis=1, keepdims=True) * (LOG2E / EPS)
     slot = lax.broadcasted_iota(jnp.int32, (slots, 1), 0)
     square = jnp.where(slot < count, square, FAR)
     square_ref[...] = jnp.broadcast_to(square, (slots, LANES))
     word_ref[...] = words.astype(jnp.bfloat16)
-    for far_ref in far_refs:
-        far_ref[...] = jnp.full(far_ref.shape, -jnp.inf, jnp.float32)
-
-    def score_step(step, carry):
-        at = pl.multiple_of(step * WIDE, WIDE)
-        for part in range(quarters):
-            half, inner = divmod(part, quarters // 2)
-            atom_ref = (own_atom_ref, other_atom_ref)[half]
-            logit_ref = (own_logit_ref, other_logit_ref)[half]
-            score_ref, far_ref = score_refs[part], far_refs[part]
-            source = pl.ds(pl.multiple_of(inner * quarter + at, WIDE), WIDE)
-            product = jnp.dot(word_ref[...], atom_ref[:, source], preferred_element_type=jnp.float32)
-            tiles = [
-                product[:, left : left + LANES] * (2.0 * LOG2E / EPS) - square_ref[...]
-                for left in range(0, WIDE, LANES)
-            ]
-            for tile, score in enumerate(tiles):
-                score_ref[:, pl.ds(at + tile * LANES, LANES)] = score
-            score = score_ref[:, pl.ds(at, WIDE)]
-            top = jnp.max(score, axis=0, keepdims=True)
-            total = jnp.sum(jnp.exp2(score - top), axis=0, keepdims=True)
-            head = logit_ref[:, source] * LOG2E - top - jnp.log(total) * LOG2E
-            start_ref[:, pl.ds(pl.multiple_of(part * quarter + at, WIDE), WIDE)] = head
-            far = far_ref[...]
-            for left in range(0, WIDE, LANES):
+    far_ref[...] = jnp.full(far_ref.shape, -jnp.inf, jnp.float32)
+    atoms = all_atoms // 2
+    chunks = all_atoms // WIDE
+
+    def multiply(chunk):
+        half, left = divmod(chunk * WIDE, atoms)
+        atom_ref = (own_atom_ref, other_atom_ref)[half]
+        product = jnp.dot(
+            word_ref[...], atom_ref[:, left : left + WIDE], preferred_element_type=jnp.float32
+        )
+        tops = []
+        for inner in range(0, WIDE, LANES):
+            at = chunk * WIDE + inner
+            score = product[:, inner : inner + LANES] * (2.0 * LOG2E / EPS) - square_ref[...]
+            score_ref[:, at : at + LANES] = score
+            tops.append(jnp.max(score, axis=0, keepdims=True))
+        return tops
+
+    def finish(chunk, tops):
+        half, left = divmod(chunk * WIDE, atoms)
+        logit_ref = (own_logit_ref, other_logit_ref)[half]
+        totals = []
+        for tile, top in enumerate(tops):
+            at = chunk * WIDE + tile * LANES
+            share = jnp.exp2(score_ref[:, at : at + LANES] - top)
+            totals.append(jnp.sum(share, axis=0, keepdims=True))
+        top = jnp.concatenate(tops, axis=1)
+        total = jnp.concatenate(totals, axis=1)
+        head = logit_ref[:, left : left + WIDE] * LOG2E - top - jnp.log(total) * LOG2E
+        start_ref[:, chunk * WIDE : (chunk + 1) * WIDE] = head
+
+    def reach(chunk, some):
+        for group in range(slots // 8):
+            lines = slice(group * 8, group * 8 + 8)
+            far = far_ref[lines, :]
+            for left in range(chunk * WIDE, (chunk + some) * WIDE, LANES):
                 far = jnp.maximum(
-                    far, score_ref[:, pl.ds(at + left, LANES)] + head[:, left : left + LANES]
+                    far, score_ref[lines, left : left + LANES] + start_ref[:, left : left + LANES]
                 )
-            far_ref[...] = far
-        return carry
-
-    lax.fori_loop(0, quarter // WIDE, score_step, 0)
+            far_ref[lines, :] = far
+
+    waiting = multiply(0)
+    for chunk in range(1, chunks):
+        coming = multiply(chunk)
+        finish(chunk - 1, waiting)
+        if chunk % 4 == 1 and chunk > 4:
+            reach(chunk - 5, 4)
+        waiting = coming
+    finish(chunks - 1, waiting)
+    reach(chunks - 4, 4)
     head_ref[...] = jnp.broadcast_to(start_ref[...], (8, all_atoms))
     for block in range(blocks):
         span = slice(block * LANES, (block + 1) * LANES)
-        far = far_refs[0][span, :]
-        for far_ref in far_refs[1:]:
-            far = jnp.maximum(far, far_ref[span, :])
-        peak = jnp.max(far, axis=1, keepdims=True)
+        peak = jnp.max(far_ref[span, :], axis=1, keepdims=True)
         near_ref[span, :] = jnp.broadcast_to(peak, (LANES, LANES))
         peak_ref[:, span] = rowify(peak, eye)
 
     def plan_step(step, carry):
-        for group in range(2):
-            at = pl.multiple_of(step * 32 + group * 16, 16)
+        for group in range(4):
+            at = pl.multiple_of(step * 64 + group * 16, 16)
             masses = [jnp.zeros((8, LANES), jnp.float32) for _ in range(2)]
             near = [near_ref[pl.ds(at + 8 * side, 8), :] for side in range(2)]
             for left in range(0, all_atoms, LANES):
-                part, inner = divmod(left, quarter)
                 shares = []
                 for side in range(2):
-                    score = score_refs[part][pl.ds(at + 8 * side, 8), inner : inner + LANES]
+                    score = score_ref[pl.ds(at + 8 * side, 8), left : left + LANES]
                     share = jnp.exp2(score + head_ref[:, left : left + LANES] - near[side])
                     masses[side] += share
                     shares.append(share)
@@ -174,7 +227,7 @@
                 mass_ref[pl.ds(at + 8 * side, 8), :] = masses[side]
         return carry
 
-    lax.fori_loop(0, slots // 32, plan_step, 0)
+    lax.fori_loop(0, slots // 64, plan_step, 0)
     copies = sent_ref.shape[0]
     for block in range(blocks):
         span = slice(block * LANES, (block + 1) * LANES)
@@ -225,9 +278,10 @@
     scale_ref[...] = scale
     base_ref[...] = (2.0 * EPS * LN2) * whole - EPS * jnp.log(words) - (EPS * LN2) * extent
     weights = pieces(scale)
-    part = jnp.zeros((8, slots), jnp.float32)
     wide = min(512, atoms)
-    for left in range(0, all_atoms, wide):
+    lefts = list(range(0, all_atoms, wide))
+
+    def gain_of(left):
         half, inner = divmod(left, atoms)
         logit_ref = (own_logit_ref, other_logit_ref)[half]
         col_ref = (own_col_ref, other_col_ref)[half]
@@ -237,10 +291,20 @@
         col_ref[:, inner : inner + wide] = EPS * (
             LN2 * start_ref[:, left : left + wide] + gain_log
         ) - (2.0 * EPS * LN2) * whole
-        part += lax.dot_general(
-            pieces(jnp.exp(gain_log)), plan_ref[:, left : left + wide], NT,
-            preferred_element_type=jnp.float32,
+        return pieces(jnp.exp(gain_log))
+
+    def row_sums(left, gain):
+        return lax.dot_general(
+            gain, plan_ref[:, left : left + wide], NT, preferred_element_type=jnp.float32
         )
+
+    part = jnp.zeros((8, slots), jnp.float32)
+    waiting = gain_of(lefts[0])
+    for spot in range(1, len(lefts)):
+        coming = gain_of(lefts[spot])
+        part += row_sums(lefts[spot - 1], waiting)
+        waiting = coming
+    part += row_sums(lefts[-1], waiting)
     part = jnp.sum(part, axis=0, keepdims=True) * scale
     for copy in range(copies):
         sent_ref[copy] = part
@@ -338,18 +402,27 @@
         ),
         [SMEM, VMEM, VMEM],
         limit=8,
-    )(core, word_shard.reshape(1, slots), word_row.reshape(1, slots))
+    )(core, word_shard.reshape(1, slots), word_row)
     asked = swap(requests.reshape(groups, 1, HALF), "docs")
     own_atoms = support_atoms.T
     other_atoms = lax.ppermute(own_atoms, "supp", pairs)
     own_logits = weight_logits.reshape(1, atoms)
     other_logits = lax.ppermute(own_logits, "supp", pairs)
-    found = vocab_table[asked.reshape(groups * HALF)]
-    own = swap(found.reshape(groups, HALF, width), "docs").reshape(groups * HALF, width)
+    found = call(
+        lookup_kernel,
+        jax.ShapeDtypeStruct((groups * HALF, TILES * LANES), jnp.bfloat16),
+        [SMEM, VMEM],
+        [
+            pltpu.VMEM(((vocab_table.shape[0] + 8) // 8 * 8 * TILES, LANES), jnp.float32),
+            pltpu.VMEM((groups * HALF * TILES + 8, LANES), jnp.float32),
+        ],
+        limit=24,
+    )(asked, vocab_table.T)
+    own = swap(found.reshape(groups, HALF, TILES * LANES), "docs")
+    own = own.reshape(groups * HALF, TILES * LANES)
+    own, other_logits = lax.optimization_barrier((own, other_logits))
     other = lax.ppermute(own, "supp", pairs)
 
-    quarters = 4
-    quarter = 2 * atoms // quarters
     plan, extent, peak, start = call(
         first_kernel,
         (
@@ -363,8 +436,8 @@
             pltpu.VMEM((doc_slots, 2 * groups * HALF), jnp.bfloat16),
             pltpu.VMEM((doc_slots, width), jnp.bfloat16),
             pltpu.VMEM((doc_slots, LANES), jnp.float32),
-            [pltpu.VMEM((doc_slots, quarter), jnp.float32)] * quarters,
-            [pltpu.VMEM((doc_slots, LANES), jnp.float32)] * quarters,
+            pltpu.VMEM((doc_slots, 2 * atoms), jnp.float32),
+            pltpu.VMEM((doc_slots, LANES), jnp.float32),
             pltpu.VMEM((8, 2 * atoms), jnp.float32),
             pltpu.VMEM((doc_slots, LANES), jnp.float32),
             pltpu.VMEM((doc_slots, LANES), jnp.float32),

time: 148 us -> 132 us (0.89)
  local copies, waits for them, and re-layouts: 16.6 us -> 3.57 us
  waiting for transfers between devices: 9.73 us -> 15.5 us
  blocking collectives: 74.2 us -> 69 us
  Pallas kernels: 22.4 us -> 20.7 us
    gather x1 -> x0, local copies, waits for them, and re-layouts: 6.85 us -> none  [shards(): found = vocab_table[asked.reshape(groups * HALF)]]
    all_to_all x4, blocking collectives: 74.2 us -> 69 us  [swap(): lax.all_to_all(x, axis, split_axis=0, concat_axis=0, tiled=True, axis_ind...]
    pallas_call x1, Pallas kernels: 13.6 us -> 8.65 us  [shards(): call(first_kernel, (jax.ShapeDtypeStruct((doc_slots, 2 * atoms), jnp.bflo...]
    pallas_call x0 -> x1, Pallas kernels: none -> 4.66 us  [shards(): call(lookup_kernel, jax.ShapeDtypeStruct((groups * HALF, TILES * LANES),...]
    unnamed x9 -> x12, local copies, waits for them, and re-layouts: 7.82 us -> 3.57 us
    all_to_all x2, starting transfers between devices: 11.2 us -> 7.26 us  [swap(): lax.all_to_all(x, axis, split_axis=0, concat_axis=0, tiled=True, axis_ind...]
    all_to_all x2, waiting for transfers between devices: 8.14 us -> 11.7 us  [swap(): lax.all_to_all(x, axis, split_axis=0, concat_axis=0, tiled=True, axis_ind...]
    ppermute x1, starting transfers between devices: 3.06 us -> 5.54 us  [shards(): other = lax.ppermute(own, 'supp', pairs)]
  transfers between devices with their start and end apart: 6 -> 6, of which waited for: 3 -> 5; matrix products, arithmetic and copies ran while one was open for 11% -> 0% of each run, Pallas kernels for 0% -> 1%
where the time goes in v3:
time: 132 us
  blocking collectives  69 us (52%)
  starting transfers between devices  22 us (17%)
  Pallas kernels  20.7 us (16%)
  waiting for transfers between devices  15.5 us (12%)
  local copies, waits for them, and re-layouts  3.57 us (3%)
    all_to_all x4, blocking collectives, swap(): lax.all_to_all(x, axis, split_axis=0, concat_axis=0, tiled=True, axis_ind...  69 us
    all_to_all x2, waiting for transfers between devices, swap(): lax.all_to_all(x, axis, split_axis=0, concat_axis=0, tiled=True, axis_ind...  11.7 us
    pallas_call x1, Pallas kernels, shards(): call(first_kernel, (jax.ShapeDtypeStruct((doc_slots, 2 * atoms), jnp.bflo...  8.65 us
    all_to_all x2, starting transfers between devices, swap(): lax.all_to_all(x, axis, split_axis=0, concat_axis=0, tiled=True, axis_ind...  7.26 us
    ppermute x1, starting transfers between devices, shards(): other = lax.ppermute(own, 'supp', pairs)  5.54 us
    ppermute x1, starting transfers between devices, shards(): other_atoms = lax.ppermute(own_atoms, 'supp', pairs)  5.07 us
    pallas_call x1, Pallas kernels, shards(): call(lookup_kernel, jax.ShapeDtypeStruct((groups * HALF, TILES * LANES),...  4.66 us
    unnamed x12, local copies, waits for them, and re-layouts  3.57 us
  transfers between devices with their start and end apart: 6, of which 5 were waited for; matrix products, arithmetic and copies ran while one was open for 0% of the time, Pallas kernels for 1%

profile of v3, /device:TPU:1, one launch (start us, length us, event | category | flops | bytes accessed | tf_op | source)
XLA Modules:
  0.0 131.6 jit_solution(1830802215736891516)
XLA Ops:
  0.6 0.0 copy-start
  0.6 0.0 copy-start.3
  0.7 0.8 copy-done.3
  1.4 0.0 copy-start.4
  1.4 0.7 copy-done.4
  2.1 0.9 shard_map.85
  3.0 13.8 %all_to_all.30.asked_ref = s32[16,1,64]{2,1,0:T(1,128)S(1)} all-to-all(s32[16,1,64]{2,1,0:T(1,128)S(1)} %bitcast.18), channel_id=1, replica_groups=mesh['docs'=16,'supp'=32] {'docs'}, dimensions={0} | all-to-all | bytes 8192 | tf_op jit(solution)/shard_map/all_to_all | solution.py:377
  16.8 0.0 copy-start.1
  16.8 2.1 %copy-done.1 = bf16[6250,300]{0,1:T(8,128)(2,1)S(1)} copy-done((bf16[6250,300]{0,1:T(8,128)(2,1)S(1)}, bf16[6250,300]{0,1:T(8,128)(2,1)}, u32[]{:S(2)}) %copy-start.1) | copy-done | bytes 3750024
  18.9 0.0 copy-start.2
  18.9 0.0 copy-start.5
  18.9 4.7 %shard_map.86 = bf16[1024,384]{1,0:T(8,128)(2,1)} custom-call(s32[16,1,64]{2,1,0:T(1,128)S(1)} %all_to_all.30.asked_ref, bf16[300,6250]{1,0:T(8,128)(2,1)S(1)} %bitcast.12), custom_call_target="tpu_custom_call" | custom-call | tf_op jit(solution)/shard_map/pallas_call | solution.py:411
  23.6 3.6 %all-to-all-start.1 = ((bf16[16,64,384]{2,1,0:T(8,128)(2,1)}), bf16[16,64,384]{2,1,0:T(8,128)(2,1)S(1)}, u32[]{:S(2)}, u32[]{:S(2)}) async-start(bf16[16,64,384]{2,1,0:T(8,128)(2,1)} %bitcast.4), calls=%async_computation.1 | async-start | bytes 1572864 | tf_op jit(solution)/shard_map/all_to_all | solution.py:377
  27.2 0.0 copy-done
  27.2 5.1 %collective-permute-start.2 = (bf16[300,2048]{1,0:T(8,128)(2,1)S(1)}, bf16[300,2048]{1,0:T(8,128)(2,1)S(1)}, u32[]{:S(2)}, u32[]{:S(2)}) collective-permute-start(bf16[300,2048]{1,0:T(8,128)(2,1)S(1)} %bitcast.9), channel_id=1, source_target_pairs={{0,1},{1,0},{2,3},{3,2},{4,5},{5,4},{6,7},{7,6},{8,9},{9,8},{10,11... | collective-permute-start | bytes 3686408 | tf_op jit(solution)/shard_map/ppermute | solution.py:408
  32.3 0.0 copy-done.2
  32.3 1.9 %collective-permute-start = (f32[1,2048]{1,0:T(1,128)S(1)}, f32[1,2048]{1,0:T(1,128)S(1)}, u32[]{:S(2)}, u32[]{:S(2)}) collective-permute-start(f32[1,2048]{1,0:T(1,128)S(1)} %bitcast.15), channel_id=1, source_target_pairs={{0,1},{1,0},{2,3},{3,2},{4,5},{5,4},{6,7},{7,6},{8,9},{9,8},{10,11... | collective-permute-start | bytes 24584 | tf_op jit(solution)/shard_map/ppermute | solution.py:410
  34.2 1.1 collective-permute-done.other_logit_ref
  35.4 3.5 %all-to-all-done.1 = bf16[16,64,384]{2,1,0:T(8,128)(2,1)S(1)} async-done(((bf16[16,64,384]{2,1,0:T(8,128)(2,1)}), bf16[16,64,384]{2,1,0:T(8,128)(2,1)S(1)}, u32[]{:S(2)}, u32[]{:S(2)}) %all-to-all-start.1) | async-done | bytes 786464 | tf_op jit(solution)/shard_map/all_to_all | solution.py:377
  38.9 5.5 %collective-permute-start.1 = (bf16[1024,384]{1,0:T(8,128)(2,1)S(1)}, bf16[1024,384]{1,0:T(8,128)(2,1)S(1)}, u32[]{:S(2)}, u32[]{:S(2)}) collective-permute-start(bf16[1024,384]{1,0:T(8,128)(2,1)S(1)} %bitcast.13), channel_id=1, source_target_pairs={{0,1},{1,0},{2,3},{3,2},{4,5},{5,4},{6,7},{7,6},{8,9},{9,8},{10,11... | collective-permute-start | bytes 2359304 | tf_op jit(solution)/shard_map/ppermute | solution.py:424
  44.5 0.0 collective-permute-done.2.other_atom_ref
  44.5 1.9 %collective-permute-done.1.other_ref = bf16[1024,384]{1,0:T(8,128)(2,1)S(1)} collective-permute-done((bf16[1024,384]{1,0:T(8,128)(2,1)S(1)}, bf16[1024,384]{1,0:T(8,128)(2,1)S(1)}, u32[]{:S(2)}, u32[]{:S(2)}) %collective-permute-start.1) | collective-permute-done | bytes 786464 | tf_op jit(solution)/shard_map/ppermute | solution.py:424
  46.3 0.0 copy-done.5
  46.3 8.6 %shard_map.87 = (bf16[640,4096]{1,0:T(8,128)(2,1)S(1)}, f32[16,1,768]{2,1,0:T(1,128)S(1)}, f32[1,640]{1,0:T(1,128)S(1)}, f32[1,4096]{1,0:T(1,128)S(1)}) custom-call(s32[1]{0:T(128)} %bitcast.core_ref, s32[2]{0:T(128)S(1)} %copy-done.5, bf16[1024,384]{1,0:T(8,128)(2,1)S(1)} %bitcast.14, bf16[1024,384]{1,0:T(8,128)(2,1)S(1)} %collective-permute-done.1.other_ref, ...), custom_call_target="tpu_custom_call" | custom-call | tf_op jit(solution)/shard_map/pallas_call | solution.py:426
  55.0 26.2 %all_to_all.31.got_ref = f32[16,1,768]{2,1,0:T(1,128)S(1)} all-to-all(f32[16,1,768]{2,1,0:T(1,128)S(1)} %get-tuple-element.27), channel_id=1, replica_groups={{0,2,4,6,8,10,12,14,16,18,20,22,24,26,28,30},{1,3,5,7,9,11,13,15,17,19,..., dimensions={0} | all-to-all | bytes 98304 | tf_op jit(solution)/shard_map/all_to_all | solution.py:377
  81.2 2.8 %shard_map.88 = (f32[16,1,640]{2,1,0:T(1,128)S(1)}, f32[1,640]{1,0:T(1,128)S(1)}, f32[1,640]{1,0:T(1,128)S(1)}, f32[1,4096]{1,0:T(1,128)S(1)}, f32[1,2048]{1,0:T(1,128)S(1)}, /*index=5*/f32[1,2048]{1,0:T(1,128)S(1)}) custom-call(s32[1]{0:T(128)} %bitcast.core_ref, s32[2]{0:T(128)S(1)} %copy-done.5, f32[16,1,768]{2,1,0:T(1,128)S(1)} %all_to_all.31.got_ref, ...), custom_call_target="tpu_custom_call" | custom-call | tf_op jit(solution)/shard_map/pallas_call | solution.py:448
  84.0 14.0 %all_to_all.32.got_ref = f32[16,1,640]{2,1,0:T(1,128)S(1)} all-to-all(f32[16,1,640]{2,1,0:T(1,128)S(1)} %get-tuple-element.31), channel_id=1, replica_groups={{0,2,4,6,8,10,12,14,16,18,20,22,24,26,28,30},{1,3,5,7,9,11,13,15,17,19,..., dimensions={0} | all-to-all | bytes 81920 | tf_op jit(solution)/shard_map/all_to_all | solution.py:377
  98.1 1.4 %shard_map.89 = (f32[32,1,2048]{2,1,0:T(1,128)S(1)}, f32[1,2688]{1,0:T(1,128)S(1)}) custom-call(s32[1]{0:T(128)} %bitcast.core_ref, s32[2]{0:T(128)S(1)} %copy-done.5, f32[16,1,640]{2,1,0:T(1,128)S(1)} %all_to_all.32.got_ref, f32[1,640]{1,0:T(1,128)S(1)} %get-tuple-element.32.scale_ref, f32[1,640]{1,0:T(1,128)S(1)} %get-tuple-element.33.base_ref, ...), custom_call_target="tpu_custom_call" | custom-call | tf_op jit(solution)/shard_map/pallas_call | solution.py:462
  99.5 14.9 %all_to_all.33.refs_0_ = f32[32,1,2048]{2,1,0:T(1,128)S(1)} all-to-all(f32[32,1,2048]{2,1,0:T(1,128)S(1)} %get-tuple-element.40), channel_id=1, replica_groups={{0,1,32,33,64,65,96,97,128,129,160,161,192,193,224,225,256,257,288,289,..., dimensions={0} | all-to-all | bytes 524288 | tf_op jit(solution)/shard_map/all_to_all | solution.py:377
  114.4 0.8 shard_map.91
  115.2 3.6 %all-to-all-start.5 = ((f32[32,1,128]{2,1,0:T(1,128)}), f32[32,1,128]{2,1,0:T(1,128)S(1)}, u32[]{:S(2)}, u32[]{:S(2)}) async-start(f32[32,1,128]{2,1,0:T(1,128)} %get-tuple-element.41), calls=%async_computation.5 | async-start | bytes 32768 | tf_op jit(solution)/shard_map/all_to_all | solution.py:377
  118.9 2.3 %collective-permute-start.3 = (f32[1,2688]{1,0:T(1,128)S(1)}, f32[1,2688]{1,0:T(1,128)S(1)}, u32[]{:S(2)}, u32[]{:S(2)}) collective-permute-start(f32[1,2688]{1,0:T(1,128)S(1)} %get-tuple-element.36.pass_ref), channel_id=1, source_target_pairs={{0,1},{1,0},{2,3},{3,2},{4,5},{5,4},{6,7},{7,6},{8,9},{9,8},{10,11... | collective-permute-start | bytes 32264 | tf_op jit(solution)/shard_map/ppermute | solution.py:469
  121.2 0.8 collective-permute-done.3.back_ref
  122.0 0.7 shard_map.90
  122.7 8.1 %all-to-all-done.5.got_ref = f32[32,1,128]{2,1,0:T(1,128)S(1)} async-done(((f32[32,1,128]{2,1,0:T(1,128)}), f32[32,1,128]{2,1,0:T(1,128)S(1)}, u32[]{:S(2)}, u32[]{:S(2)}) %all-to-all-start.5) | async-done | bytes 16416 | tf_op jit(solution)/shard_map/all_to_all | solution.py:377
  130.8 0.8 shard_map.92
Async XLA Ops:
  0.6 26.6 %copy-start = (bf16[2048,300]{0,1:T(8,128)(2,1)S(1)}, bf16[2048,300]{0,1:T(8,128)(2,1)}, u32[]{:S(2)}) copy-start(bf16[2048,300]{0,1:T(8,128)(2,1)} %param.7) | copy-start | bytes 3686404
  0.6 0.8 copy-start.3
  1.4 0.7 copy-start.4
  16.8 2.1 %copy-start.1 = (bf16[6250,300]{0,1:T(8,128)(2,1)S(1)}, bf16[6250,300]{0,1:T(8,128)(2,1)}, u32[]{:S(2)}) copy-start(bf16[6250,300]{0,1:T(8,128)(2,1)} %param.6) | copy-start | bytes 11250004
  18.9 13.4 %copy-start.2 = (f32[2048]{0:T(1024)S(1)}, f32[2048]{0:T(1024)}, u32[]{:S(2)}) copy-start(f32[2048]{0:T(1024)} %param.8) | copy-start | bytes 24580
  18.9 27.4 %copy-start.5 = (s32[2]{0:T(128)S(1)}, s32[2]{0:T(128)}, u32[]{:S(2)}) copy-start(s32[2]{0:T(128)} %count_ref.5) | copy-start | bytes 28
  23.6 15.3 %all-to-all-start.1 = ((bf16[16,64,384]{2,1,0:T(8,128)(2,1)}), bf16[16,64,384]{2,1,0:T(8,128)(2,1)S(1)}, u32[]{:S(2)}, u32[]{:S(2)}) async-start(bf16[16,64,384]{2,1,0:T(8,128)(2,1)} %bitcast.4), calls=%async_computation.1 | async-start | bytes 1572864 | tf_op jit(solution)/shard_map/all_to_all | solution.py:377
  27.2 17.2 %collective-permute-start.2 = (bf16[300,2048]{1,0:T(8,128)(2,1)S(1)}, bf16[300,2048]{1,0:T(8,128)(2,1)S(1)}, u32[]{:S(2)}, u32[]{:S(2)}) collective-permute-start(bf16[300,2048]{1,0:T(8,128)(2,1)S(1)} %bitcast.9), channel_id=1, source_target_pairs={{0,1},{1,0},{2,3},{3,2},{4,5},{5,4},{6,7},{7,6},{8,9},{9,8},{10,11... | collective-permute-start | bytes 3686408 | tf_op jit(solution)/shard_map/ppermute | solution.py:408
  32.3 3.1 %collective-permute-start = (f32[1,2048]{1,0:T(1,128)S(1)}, f32[1,2048]{1,0:T(1,128)S(1)}, u32[]{:S(2)}, u32[]{:S(2)}) collective-permute-start(f32[1,2048]{1,0:T(1,128)S(1)} %bitcast.15), channel_id=1, source_target_pairs={{0,1},{1,0},{2,3},{3,2},{4,5},{5,4},{6,7},{7,6},{8,9},{9,8},{10,11... | collective-permute-start | bytes 24584 | tf_op jit(solution)/shard_map/ppermute | solution.py:410
  38.9 7.4 %collective-permute-start.1 = (bf16[1024,384]{1,0:T(8,128)(2,1)S(1)}, bf16[1024,384]{1,0:T(8,128)(2,1)S(1)}, u32[]{:S(2)}, u32[]{:S(2)}) collective-permute-start(bf16[1024,384]{1,0:T(8,128)(2,1)S(1)} %bitcast.13), channel_id=1, source_target_pairs={{0,1},{1,0},{2,3},{3,2},{4,5},{5,4},{6,7},{7,6},{8,9},{9,8},{10,11... | collective-permute-start | bytes 2359304 | tf_op jit(solution)/shard_map/ppermute | solution.py:424
  115.2 15.6 %all-to-all-start.5 = ((f32[32,1,128]{2,1,0:T(1,128)}), f32[32,1,128]{2,1,0:T(1,128)S(1)}, u32[]{:S(2)}, u32[]{:S(2)}) async-start(f32[32,1,128]{2,1,0:T(1,128)} %get-tuple-element.41), calls=%async_computation.5 | async-start | bytes 32768 | tf_op jit(solution)/shard_map/all_to_all | solution.py:377
  118.9 3.1 %collective-permute-start.3 = (f32[1,2688]{1,0:T(1,128)S(1)}, f32[1,2688]{1,0:T(1,128)S(1)}, u32[]{:S(2)}, u32[]{:S(2)}) collective-permute-start(f32[1,2688]{1,0:T(1,128)S(1)} %get-tuple-element.36.pass_ref), channel_id=1, source_target_pairs={{0,1},{1,0},{2,3},{3,2},{4,5},{5,4},{6,7},{7,6},{8,9},{9,8},{10,11... | collective-permute-start | bytes 32264 | tf_op jit(solution)/shard_map/ppermute | solution.py:469

commit v4 on v3

--- a/solution.py
+++ b/solution.py
@@ -49,7 +49,11 @@
     return jnp.sum(jnp.where(eye, row, 0.0), axis=1, keepdims=True)
 
 
-def request_kernel(core_ref, shard_ref, row_ref, req_ref, pos_ref):
+def request_kernel(
+    core_ref, shard_ref, row_ref, source_ref, req_ref, pos_ref, vocab_ref, sem,
+):
+    vocab_copy = pltpu.make_async_copy(source_ref, vocab_ref, sem)
+    vocab_copy.start()
     groups = req_ref.shape[0]
     slots = shard_ref.shape[1]
     doc_slots = pos_ref.shape[1]
@@ -83,6 +87,7 @@
     for block in range(own_blocks):
         span = slice(block * LANES, (block + 1) * LANES)
         pos_ref[:, span] = jnp.where(core == 0, places[block], places[own_blocks + block])
+    vocab_copy.wait()
 
 
 def lookup_kernel(asked_ref, vocab_ref, found_ref, table_ref, line_ref):
@@ -90,16 +95,10 @@
     groups = asked_ref.shape[0]
     seats = asked_ref.shape[2]
     count = found_ref.shape[0]
-    sides = lax.broadcasted_iota(jnp.int32, (WIDE, WIDE), 0)
-    same = (sides == lax.broadcasted_iota(jnp.int32, (WIDE, WIDE), 1)).astype(jnp.float32)
-    same = same.astype(jnp.bfloat16)
     tiles = [(tile, min(LANES, width - tile * LANES)) for tile in range(TILES)]
 
     def spread(first, some):
-        turned = lax.dot_general(
-            same[:some, :some], vocab_ref[:, pl.ds(first, some)], NT,
-            preferred_element_type=jnp.float32,
-        )
+        turned = vocab_ref[:, pl.ds(first, some)].astype(jnp.float32).T
         for tile, lanes in tiles:
             left = tile * LANES
             table_ref[pl.ds(first * TILES + tile, some, stride=TILES), :lanes] = turned[
@@ -394,15 +393,17 @@
         for level in range(0, parts, 2)
     ]
 
-    requests, place = call(
+    requests, place, vocab = call(
         request_kernel,
         (
             jax.ShapeDtypeStruct((groups, HALF), jnp.int32),
             jax.ShapeDtypeStruct((1, doc_slots), jnp.int32),
+            jax.ShapeDtypeStruct(vocab_table.shape[::-1], vocab_table.dtype),
         ),
-        [SMEM, VMEM, VMEM],
-        limit=8,
-    )(core, word_shard.reshape(1, slots), word_row)
+        [SMEM, VMEM, VMEM, pl.BlockSpec(memory_space=pltpu.HBM)],
+        [pltpu.SemaphoreType.DMA],
+        limit=48,
+    )(core, word_shard.reshape(1, slots), word_row, vocab_table.T)
     asked = swap(requests.reshape(groups, 1, HALF), "docs")
     own_atoms = support_atoms.T
     other_atoms = lax.ppermute(own_atoms, "supp", pairs)
@@ -417,7 +418,7 @@
             pltpu.VMEM((groups * HALF * TILES + 8, LANES), jnp.float32),
         ],
         limit=24,
-    )(asked, vocab_table.T)
+    )(asked, vocab)
     own = swap(found.reshape(groups, HALF, TILES * LANES), "docs")
     own = own.reshape(groups * HALF, TILES * LANES)
     own, other_logits = lax.optimization_barrier((own, other_logits))

time: 132 us -> 131 us (level)
  local copies, waits for them, and re-layouts: 3.57 us -> 1.4 us
    unnamed x12 -> x10, local copies, waits for them, and re-layouts: 3.57 us -> 1.4 us
where the time goes in v4:
time: 131 us; the launch traced here: 130 us
  blocking collectives  69.1 us (53%)
  starting transfers between devices  22 us (17%)
  Pallas kernels  21.4 us (16%)
  waiting for transfers between devices  15.5 us (12%)
  local copies, waits for them, and re-layouts  1.4 us (1%)
    all_to_all x4, blocking collectives, swap(): lax.all_to_all(x, axis, split_axis=0, concat_axis=0, tiled=True, axis_ind...  69.1 us
    all_to_all x2, waiting for transfers between devices, swap(): lax.all_to_all(x, axis, split_axis=0, concat_axis=0, tiled=True, axis_ind...  11.7 us
    pallas_call x1, Pallas kernels, shards(): call(first_kernel, (jax.ShapeDtypeStruct((doc_slots, 2 * atoms), jnp.bflo...  8.64 us
    all_to_all x2, starting transfers between devices, swap(): lax.all_to_all(x, axis, split_axis=0, concat_axis=0, tiled=True, axis_ind...  7.26 us
    ppermute x1, starting transfers between devices, shards(): other = lax.ppermute(own, 'supp', pairs)  5.54 us
    ppermute x1, starting transfers between devices, shards(): other_atoms = lax.ppermute(own_atoms, 'supp', pairs)  5.07 us
    pallas_call x1, Pallas kernels, shards(): call(lookup_kernel, jax.ShapeDtypeStruct((groups * HALF, TILES * LANES),...  4.17 us
    pallas_call x1, Pallas kernels, shards(): call(second_kernel, (f32((parts // 2, 1, doc_slots)), f32((1, doc_slots))...  2.82 us
  transfers between devices with their start and end apart: 6, of which 5 were waited for; matrix products, arithmetic and copies ran while one was open for 0% of the time, Pallas kernels for 1%

profile of v4, /device:TPU:1, one launch (start us, length us, event | category | flops | bytes accessed | tf_op | source)
XLA Modules:
  0.0 130.2 jit_solution(10541800441629870717)
XLA Ops:
  0.6 0.0 copy-start.2
  0.6 0.7 copy-done.2
  1.3 0.0 copy-start.3
  1.3 0.7 copy-done.3
  2.0 2.1 %shard_map.85 = (s32[16,64]{1,0:T(8,128)S(1)}, s32[1,640]{1,0:T(1,128)S(1)}, bf16[300,6250]{1,0:T(8,128)(2,1)S(1)}) custom-call(s32[1]{0:T(128)} %bitcast.core_ref, s32[1,1280]{1,0:T(1,128)S(1)} %bitcast.18, s32[1280]{0:T(1024)S(1)} %copy-done.2, bf16[300,6250]{1,0:T(8,128)(2,1)} %bitcast.19), custom_call_target="tpu_custom_call" | custom-call | tf_op jit(solution)/shard_map/pallas_call | solution.py:396
  4.1 0.0 copy-start
  4.1 0.0 copy-start.1
  4.1 0.0 copy-start.4
  4.2 13.9 %all_to_all.30.asked_ref = s32[16,1,64]{2,1,0:T(1,128)S(1)} all-to-all(s32[16,1,64]{2,1,0:T(1,128)S(1)} %bitcast.17), channel_id=1, replica_groups=mesh['docs'=16,'supp'=32] {'docs'}, dimensions={0} | all-to-all | bytes 8192 | tf_op jit(solution)/shard_map/all_to_all | solution.py:376
  18.1 4.2 %shard_map.86 = bf16[1024,384]{1,0:T(8,128)(2,1)} custom-call(s32[16,1,64]{2,1,0:T(1,128)S(1)} %all_to_all.30.asked_ref, bf16[300,6250]{1,0:T(8,128)(2,1)S(1)} %get-tuple-element.25.vocab_ref), custom_call_target="tpu_custom_call" | custom-call | tf_op jit(solution)/shard_map/pallas_call | solution.py:412
  22.3 3.6 %all-to-all-start.1 = ((bf16[16,64,384]{2,1,0:T(8,128)(2,1)}), bf16[16,64,384]{2,1,0:T(8,128)(2,1)S(1)}, u32[]{:S(2)}, u32[]{:S(2)}) async-start(bf16[16,64,384]{2,1,0:T(8,128)(2,1)} %bitcast.4), calls=%async_computation.1 | async-start | bytes 1572864 | tf_op jit(solution)/shard_map/all_to_all | solution.py:376
  25.9 0.0 copy-done
  25.9 5.1 %collective-permute-start.2 = (bf16[300,2048]{1,0:T(8,128)(2,1)S(1)}, bf16[300,2048]{1,0:T(8,128)(2,1)S(1)}, u32[]{:S(2)}, u32[]{:S(2)}) collective-permute-start(bf16[300,2048]{1,0:T(8,128)(2,1)S(1)} %bitcast.9), channel_id=1, source_target_pairs={{0,1},{1,0},{2,3},{3,2},{4,5},{5,4},{6,7},{7,6},{8,9},{9,8},{10,11... | collective-permute-start | bytes 3686408 | tf_op jit(solution)/shard_map/ppermute | solution.py:409
  31.0 0.0 copy-done.1
  31.0 1.9 %collective-permute-start = (f32[1,2048]{1,0:T(1,128)S(1)}, f32[1,2048]{1,0:T(1,128)S(1)}, u32[]{:S(2)}, u32[]{:S(2)}) collective-permute-start(f32[1,2048]{1,0:T(1,128)S(1)} %bitcast.14), channel_id=1, source_target_pairs={{0,1},{1,0},{2,3},{3,2},{4,5},{5,4},{6,7},{7,6},{8,9},{9,8},{10,11... | collective-permute-start | bytes 24584 | tf_op jit(solution)/shard_map/ppermute | solution.py:411
  32.9 1.1 collective-permute-done.other_logit_ref
  34.0 3.5 %all-to-all-done.1 = bf16[16,64,384]{2,1,0:T(8,128)(2,1)S(1)} async-done(((bf16[16,64,384]{2,1,0:T(8,128)(2,1)}), bf16[16,64,384]{2,1,0:T(8,128)(2,1)S(1)}, u32[]{:S(2)}, u32[]{:S(2)}) %all-to-all-start.1) | async-done | bytes 786464 | tf_op jit(solution)/shard_map/all_to_all | solution.py:376
  37.6 5.5 %collective-permute-start.1 = (bf16[1024,384]{1,0:T(8,128)(2,1)S(1)}, bf16[1024,384]{1,0:T(8,128)(2,1)S(1)}, u32[]{:S(2)}, u32[]{:S(2)}) collective-permute-start(bf16[1024,384]{1,0:T(8,128)(2,1)S(1)} %bitcast.12), channel_id=1, source_target_pairs={{0,1},{1,0},{2,3},{3,2},{4,5},{5,4},{6,7},{7,6},{8,9},{9,8},{10,11... | collective-permute-start | bytes 2359304 | tf_op jit(solution)/shard_map/ppermute | solution.py:425
  43.1 0.0 collective-permute-done.2.other_atom_ref
  43.1 1.9 %collective-permute-done.1.other_ref = bf16[1024,384]{1,0:T(8,128)(2,1)S(1)} collective-permute-done((bf16[1024,384]{1,0:T(8,128)(2,1)S(1)}, bf16[1024,384]{1,0:T(8,128)(2,1)S(1)}, u32[]{:S(2)}, u32[]{:S(2)}) %collective-permute-start.1) | collective-permute-done | bytes 786464 | tf_op jit(solution)/shard_map/ppermute | solution.py:425
  45.0 0.0 copy-done.4
  45.0 8.6 %shard_map.87 = (bf16[640,4096]{1,0:T(8,128)(2,1)S(1)}, f32[16,1,768]{2,1,0:T(1,128)S(1)}, f32[1,640]{1,0:T(1,128)S(1)}, f32[1,4096]{1,0:T(1,128)S(1)}) custom-call(s32[1]{0:T(128)} %bitcast.core_ref, s32[2]{0:T(128)S(1)} %copy-done.4, bf16[1024,384]{1,0:T(8,128)(2,1)S(1)} %bitcast.13, bf16[1024,384]{1,0:T(8,128)(2,1)S(1)} %collective-permute-done.1.other_ref, ...), custom_call_target="tpu_custom_call" | custom-call | tf_op jit(solution)/shard_map/pallas_call | solution.py:427
  53.7 26.2 %all_to_all.31.got_ref = f32[16,1,768]{2,1,0:T(1,128)S(1)} all-to-all(f32[16,1,768]{2,1,0:T(1,128)S(1)} %get-tuple-element.29), channel_id=1, replica_groups={{0,2,4,6,8,10,12,14,16,18,20,22,24,26,28,30},{1,3,5,7,9,11,13,15,17,19,..., dimensions={0} | all-to-all | bytes 98304 | tf_op jit(solution)/shard_map/all_to_all | solution.py:376
  79.9 2.8 %shard_map.88 = (f32[16,1,640]{2,1,0:T(1,128)S(1)}, f32[1,640]{1,0:T(1,128)S(1)}, f32[1,640]{1,0:T(1,128)S(1)}, f32[1,4096]{1,0:T(1,128)S(1)}, f32[1,2048]{1,0:T(1,128)S(1)}, /*index=5*/f32[1,2048]{1,0:T(1,128)S(1)}) custom-call(s32[1]{0:T(128)} %bitcast.core_ref, s32[2]{0:T(128)S(1)} %copy-done.4, f32[16,1,768]{2,1,0:T(1,128)S(1)} %all_to_all.31.got_ref, ...), custom_call_target="tpu_custom_call" | custom-call | tf_op jit(solution)/shard_map/pallas_call | solution.py:449
  82.7 14.0 %all_to_all.32.got_ref = f32[16,1,640]{2,1,0:T(1,128)S(1)} all-to-all(f32[16,1,640]{2,1,0:T(1,128)S(1)} %get-tuple-element.33), channel_id=1, replica_groups={{0,2,4,6,8,10,12,14,16,18,20,22,24,26,28,30},{1,3,5,7,9,11,13,15,17,19,..., dimensions={0} | all-to-all | bytes 81920 | tf_op jit(solution)/shard_map/all_to_all | solution.py:376
  96.8 1.4 %shard_map.89 = (f32[32,1,2048]{2,1,0:T(1,128)S(1)}, f32[1,2688]{1,0:T(1,128)S(1)}) custom-call(s32[1]{0:T(128)} %bitcast.core_ref, s32[2]{0:T(128)S(1)} %copy-done.4, f32[16,1,640]{2,1,0:T(1,128)S(1)} %all_to_all.32.got_ref, f32[1,640]{1,0:T(1,128)S(1)} %get-tuple-element.34.scale_ref, f32[1,640]{1,0:T(1,128)S(1)} %get-tuple-element.35.base_ref, ...), custom_call_target="tpu_custom_call" | custom-call | tf_op jit(solution)/shard_map/pallas_call | solution.py:463
  98.2 14.9 %all_to_all.33.refs_0_ = f32[32,1,2048]{2,1,0:T(1,128)S(1)} all-to-all(f32[32,1,2048]{2,1,0:T(1,128)S(1)} %get-tuple-element.42), channel_id=1, replica_groups={{0,1,32,33,64,65,96,97,128,129,160,161,192,193,224,225,256,257,288,289,..., dimensions={0} | all-to-all | bytes 524288 | tf_op jit(solution)/shard_map/all_to_all | solution.py:376
  113.1 0.8 shard_map.91
  113.9 3.6 %all-to-all-start.5 = ((f32[32,1,128]{2,1,0:T(1,128)}), f32[32,1,128]{2,1,0:T(1,128)S(1)}, u32[]{:S(2)}, u32[]{:S(2)}) async-start(f32[32,1,128]{2,1,0:T(1,128)} %get-tuple-element.43), calls=%async_computation.5 | async-start | bytes 32768 | tf_op jit(solution)/shard_map/all_to_all | solution.py:376
  117.5 2.3 %collective-permute-start.3 = (f32[1,2688]{1,0:T(1,128)S(1)}, f32[1,2688]{1,0:T(1,128)S(1)}, u32[]{:S(2)}, u32[]{:S(2)}) collective-permute-start(f32[1,2688]{1,0:T(1,128)S(1)} %get-tuple-element.38.pass_ref), channel_id=1, source_target_pairs={{0,1},{1,0},{2,3},{3,2},{4,5},{5,4},{6,7},{7,6},{8,9},{9,8},{10,11... | collective-permute-start | bytes 32264 | tf_op jit(solution)/shard_map/ppermute | solution.py:470
  119.8 0.8 collective-permute-done.3.back_ref
  120.6 0.7 shard_map.90
  121.3 8.1 %all-to-all-done.5.got_ref = f32[32,1,128]{2,1,0:T(1,128)S(1)} async-done(((f32[32,1,128]{2,1,0:T(1,128)}), f32[32,1,128]{2,1,0:T(1,128)S(1)}, u32[]{:S(2)}, u32[]{:S(2)}) %all-to-all-start.5) | async-done | bytes 16416 | tf_op jit(solution)/shard_map/all_to_all | solution.py:376
  129.5 0.8 shard_map.92
Async XLA Ops:
  0.6 0.7 copy-start.2
  1.3 0.7 copy-start.3
  4.1 21.8 %copy-start = (bf16[2048,300]{0,1:T(8,128)(2,1)S(1)}, bf16[2048,300]{0,1:T(8,128)(2,1)}, u32[]{:S(2)}) copy-start(bf16[2048,300]{0,1:T(8,128)(2,1)} %param.7) | copy-start | bytes 3686404
  4.1 26.8 %copy-start.1 = (f32[2048]{0:T(1024)S(1)}, f32[2048]{0:T(1024)}, u32[]{:S(2)}) copy-start(f32[2048]{0:T(1024)} %param.8) | copy-start | bytes 24580
  4.1 40.9 %copy-start.4 = (s32[2]{0:T(128)S(1)}, s32[2]{0:T(128)}, u32[]{:S(2)}) copy-start(s32[2]{0:T(128)} %count_ref.5) | copy-start | bytes 28
  22.3 15.3 %all-to-all-start.1 = ((bf16[16,64,384]{2,1,0:T(8,128)(2,1)}), bf16[16,64,384]{2,1,0:T(8,128)(2,1)S(1)}, u32[]{:S(2)}, u32[]{:S(2)}) async-start(bf16[16,64,384]{2,1,0:T(8,128)(2,1)} %bitcast.4), calls=%async_computation.1 | async-start | bytes 1572864 | tf_op jit(solution)/shard_map/all_to_all | solution.py:376
  25.9 17.2 %collective-permute-start.2 = (bf16[300,2048]{1,0:T(8,128)(2,1)S(1)}, bf16[300,2048]{1,0:T(8,128)(2,1)S(1)}, u32[]{:S(2)}, u32[]{:S(2)}) collective-permute-start(bf16[300,2048]{1,0:T(8,128)(2,1)S(1)} %bitcast.9), channel_id=1, source_target_pairs={{0,1},{1,0},{2,3},{3,2},{4,5},{5,4},{6,7},{7,6},{8,9},{9,8},{10,11... | collective-permute-start | bytes 3686408 | tf_op jit(solution)/shard_map/ppermute | solution.py:409
  31.0 3.1 %collective-permute-start = (f32[1,2048]{1,0:T(1,128)S(1)}, f32[1,2048]{1,0:T(1,128)S(1)}, u32[]{:S(2)}, u32[]{:S(2)}) collective-permute-start(f32[1,2048]{1,0:T(1,128)S(1)} %bitcast.14), channel_id=1, source_target_pairs={{0,1},{1,0},{2,3},{3,2},{4,5},{5,4},{6,7},{7,6},{8,9},{9,8},{10,11... | collective-permute-start | bytes 24584 | tf_op jit(solution)/shard_map/ppermute | solution.py:411
  37.6 7.4 %collective-permute-start.1 = (bf16[1024,384]{1,0:T(8,128)(2,1)S(1)}, bf16[1024,384]{1,0:T(8,128)(2,1)S(1)}, u32[]{:S(2)}, u32[]{:S(2)}) collective-permute-start(bf16[1024,384]{1,0:T(8,128)(2,1)S(1)} %bitcast.12), channel_id=1, source_target_pairs={{0,1},{1,0},{2,3},{3,2},{4,5},{5,4},{6,7},{7,6},{8,9},{9,8},{10,11... | collective-permute-start | bytes 2359304 | tf_op jit(solution)/shard_map/ppermute | solution.py:425
  113.9 15.6 %all-to-all-start.5 = ((f32[32,1,128]{2,1,0:T(1,128)}), f32[32,1,128]{2,1,0:T(1,128)S(1)}, u32[]{:S(2)}, u32[]{:S(2)}) async-start(f32[32,1,128]{2,1,0:T(1,128)} %get-tuple-element.43), calls=%async_computation.5 | async-start | bytes 32768 | tf_op jit(solution)/shard_map/all_to_all | solution.py:376
  117.5 3.1 %collective-permute-start.3 = (f32[1,2688]{1,0:T(1,128)S(1)}, f32[1,2688]{1,0:T(1,128)S(1)}, u32[]{:S(2)}, u32[]{:S(2)}) collective-permute-start(f32[1,2688]{1,0:T(1,128)S(1)} %get-tuple-element.38.pass_ref), channel_id=1, source_target_pairs={{0,1},{1,0},{2,3},{3,2},{4,5},{5,4},{6,7},{7,6},{8,9},{9,8},{10,11... | collective-permute-start | bytes 32264 | tf_op jit(solution)/shard_map/ppermute | solution.py:470

commit v5 on v4

--- a/solution.py
+++ b/solution.py
@@ -14,6 +14,7 @@
 LANES = 128
 FAR = 1e30
 WIDE = 256
+CHUNK = 512
 TILES = 3
 VMEM = pl.BlockSpec(memory_space=pltpu.VMEM)
 SMEM = pl.BlockSpec(memory_space=pltpu.SMEM)
@@ -152,40 +153,40 @@
     word_ref[...] = words.astype(jnp.bfloat16)
     far_ref[...] = jnp.full(far_ref.shape, -jnp.inf, jnp.float32)
     atoms = all_atoms // 2
-    chunks = all_atoms // WIDE
+    chunks = all_atoms // CHUNK
 
     def multiply(chunk):
-        half, left = divmod(chunk * WIDE, atoms)
+        half, left = divmod(chunk * CHUNK, atoms)
         atom_ref = (own_atom_ref, other_atom_ref)[half]
         product = jnp.dot(
-            word_ref[...], atom_ref[:, left : left + WIDE], preferred_element_type=jnp.float32
+            word_ref[...], atom_ref[:, left : left + CHUNK], preferred_element_type=jnp.float32
         )
         tops = []
-        for inner in range(0, WIDE, LANES):
-            at = chunk * WIDE + inner
+        for inner in range(0, CHUNK, LANES):
+            at = chunk * CHUNK + inner
             score = product[:, inner : inner + LANES] * (2.0 * LOG2E / EPS) - square_ref[...]
             score_ref[:, at : at + LANES] = score
             tops.append(jnp.max(score, axis=0, keepdims=True))
         return tops
 
     def finish(chunk, tops):
-        half, left = divmod(chunk * WIDE, atoms)
+        half, left = divmod(chunk * CHUNK, atoms)
         logit_ref = (own_logit_ref, other_logit_ref)[half]
         totals = []
         for tile, top in enumerate(tops):
-            at = chunk * WIDE + tile * LANES
+            at = chunk * CHUNK + tile * LANES
             share = jnp.exp2(score_ref[:, at : at + LANES] - top)
             totals.append(jnp.sum(share, axis=0, keepdims=True))
         top = jnp.concatenate(tops, axis=1)
         total = jnp.concatenate(totals, axis=1)
-        head = logit_ref[:, left : left + WIDE] * LOG2E - top - jnp.log(total) * LOG2E
-        start_ref[:, chunk * WIDE : (chunk + 1) * WIDE] = head
+        head = logit_ref[:, left : left + CHUNK] * LOG2E - top - jnp.log(total) * LOG2E
+        start_ref[:, chunk * CHUNK : (chunk + 1) * CHUNK] = head
 
     def reach(chunk, some):
         for group in range(slots // 8):
             lines = slice(group * 8, group * 8 + 8)
             far = far_ref[lines, :]
-            for left in range(chunk * WIDE, (chunk + some) * WIDE, LANES):
+            for left in range(chunk * CHUNK, (chunk + some) * CHUNK, LANES):
                 far = jnp.maximum(
                     far, score_ref[lines, left : left + LANES] + start_ref[:, left : left + LANES]
                 )
@@ -195,11 +196,11 @@
     for chunk in range(1, chunks):
         coming = multiply(chunk)
         finish(chunk - 1, waiting)
-        if chunk % 4 == 1 and chunk > 4:
-            reach(chunk - 5, 4)
+        if chunk % 2 == 1 and chunk > 2:
+            reach(chunk - 3, 2)
         waiting = coming
     finish(chunks - 1, waiting)
-    reach(chunks - 4, 4)
+    reach(chunks - 2, 2)
     head_ref[...] = jnp.broadcast_to(start_ref[...], (8, all_atoms))
     for block in range(blocks):
         span = slice(block * LANES, (block + 1) * LANES)

time: 131 us -> 131 us (level)
  no operation moved by 1% of the time
where the time goes in v5:
time: 131 us; the launch traced here: 130 us
  blocking collectives  69.1 us (53%)
  starting transfers between devices  22 us (17%)
  Pallas kernels  21.4 us (16%)
  waiting for transfers between devices  15.5 us (12%)
  local copies, waits for them, and re-layouts  1.4 us (1%)
    all_to_all x4, blocking collectives, swap(): lax.all_to_all(x, axis, split_axis=0, concat_axis=0, tiled=True, axis_ind...  69.1 us
    all_to_all x2, waiting for transfers between devices, swap(): lax.all_to_all(x, axis, split_axis=0, concat_axis=0, tiled=True, axis_ind...  11.7 us
    pallas_call x1, Pallas kernels, shards(): call(first_kernel, (jax.ShapeDtypeStruct((doc_slots, 2 * atoms), jnp.bflo...  8.67 us
    all_to_all x2, starting transfers between devices, swap(): lax.all_to_all(x, axis, split_axis=0, concat_axis=0, tiled=True, axis_ind...  7.26 us
    ppermute x1, starting transfers between devices, shards(): other = lax.ppermute(own, 'supp', pairs)  5.54 us
    ppermute x1, starting transfers between devices, shards(): other_atoms = lax.ppermute(own_atoms, 'supp', pairs)  5.07 us
    pallas_call x1, Pallas kernels, shards(): call(lookup_kernel, jax.ShapeDtypeStruct((groups * HALF, TILES * LANES),...  4.17 us
    pallas_call x1, Pallas kernels, shards(): call(second_kernel, (f32((parts // 2, 1, doc_slots)), f32((1, doc_slots))...  2.82 us
  transfers between devices with their start and end apart: 6, of which 5 were waited for; matrix products, arithmetic and copies ran while one was open for 0% of the time, Pallas kernels for 1%

profile of v5, /device:TPU:1, one launch (start us, length us, event | category | flops | bytes accessed | tf_op | source)
XLA Modules:
  0.0 130.3 jit_solution(13219593759319575837)
XLA Ops:
  0.6 0.0 copy-start.2
  0.6 0.7 copy-done.2
  1.3 0.0 copy-start.3
  1.3 0.7 copy-done.3
  2.0 2.1 %shard_map.85 = (s32[16,64]{1,0:T(8,128)S(1)}, s32[1,640]{1,0:T(1,128)S(1)}, bf16[300,6250]{1,0:T(8,128)(2,1)S(1)}) custom-call(s32[1]{0:T(128)} %bitcast.core_ref, s32[1,1280]{1,0:T(1,128)S(1)} %bitcast.18, s32[1280]{0:T(1024)S(1)} %copy-done.2, bf16[300,6250]{1,0:T(8,128)(2,1)} %bitcast.19), custom_call_target="tpu_custom_call" | custom-call | tf_op jit(solution)/shard_map/pallas_call | solution.py:397
  4.1 0.0 copy-start
  4.1 0.0 copy-start.1
  4.1 0.0 copy-start.4
  4.2 13.9 %all_to_all.30.asked_ref = s32[16,1,64]{2,1,0:T(1,128)S(1)} all-to-all(s32[16,1,64]{2,1,0:T(1,128)S(1)} %bitcast.17), channel_id=1, replica_groups=mesh['docs'=16,'supp'=32] {'docs'}, dimensions={0} | all-to-all | bytes 8192 | tf_op jit(solution)/shard_map/all_to_all | solution.py:377
  18.1 4.2 %shard_map.86 = bf16[1024,384]{1,0:T(8,128)(2,1)} custom-call(s32[16,1,64]{2,1,0:T(1,128)S(1)} %all_to_all.30.asked_ref, bf16[300,6250]{1,0:T(8,128)(2,1)S(1)} %get-tuple-element.25.vocab_ref), custom_call_target="tpu_custom_call" | custom-call | tf_op jit(solution)/shard_map/pallas_call | solution.py:413
  22.3 3.6 %all-to-all-start.1 = ((bf16[16,64,384]{2,1,0:T(8,128)(2,1)}), bf16[16,64,384]{2,1,0:T(8,128)(2,1)S(1)}, u32[]{:S(2)}, u32[]{:S(2)}) async-start(bf16[16,64,384]{2,1,0:T(8,128)(2,1)} %bitcast.4), calls=%async_computation.1 | async-start | bytes 1572864 | tf_op jit(solution)/shard_map/all_to_all | solution.py:377
  25.9 0.0 copy-done
  25.9 5.1 %collective-permute-start.2 = (bf16[300,2048]{1,0:T(8,128)(2,1)S(1)}, bf16[300,2048]{1,0:T(8,128)(2,1)S(1)}, u32[]{:S(2)}, u32[]{:S(2)}) collective-permute-start(bf16[300,2048]{1,0:T(8,128)(2,1)S(1)} %bitcast.9), channel_id=1, source_target_pairs={{0,1},{1,0},{2,3},{3,2},{4,5},{5,4},{6,7},{7,6},{8,9},{9,8},{10,11... | collective-permute-start | bytes 3686408 | tf_op jit(solution)/shard_map/ppermute | solution.py:410
  31.0 0.0 copy-done.1
  31.0 1.9 %collective-permute-start = (f32[1,2048]{1,0:T(1,128)S(1)}, f32[1,2048]{1,0:T(1,128)S(1)}, u32[]{:S(2)}, u32[]{:S(2)}) collective-permute-start(f32[1,2048]{1,0:T(1,128)S(1)} %bitcast.14), channel_id=1, source_target_pairs={{0,1},{1,0},{2,3},{3,2},{4,5},{5,4},{6,7},{7,6},{8,9},{9,8},{10,11... | collective-permute-start | bytes 24584 | tf_op jit(solution)/shard_map/ppermute | solution.py:412
  32.9 1.1 collective-permute-done.other_logit_ref
  34.0 3.5 %all-to-all-done.1 = bf16[16,64,384]{2,1,0:T(8,128)(2,1)S(1)} async-done(((bf16[16,64,384]{2,1,0:T(8,128)(2,1)}), bf16[16,64,384]{2,1,0:T(8,128)(2,1)S(1)}, u32[]{:S(2)}, u32[]{:S(2)}) %all-to-all-start.1) | async-done | bytes 786464 | tf_op jit(solution)/shard_map/all_to_all | solution.py:377
  37.6 5.5 %collective-permute-start.1 = (bf16[1024,384]{1,0:T(8,128)(2,1)S(1)}, bf16[1024,384]{1,0:T(8,128)(2,1)S(1)}, u32[]{:S(2)}, u32[]{:S(2)}) collective-permute-start(bf16[1024,384]{1,0:T(8,128)(2,1)S(1)} %bitcast.12), channel_id=1, source_target_pairs={{0,1},{1,0},{2,3},{3,2},{4,5},{5,4},{6,7},{7,6},{8,9},{9,8},{10,11... | collective-permute-start | bytes 2359304 | tf_op jit(solution)/shard_map/ppermute | solution.py:426
  43.1 0.0 collective-permute-done.2.other_atom_ref
  43.1 1.9 %collective-permute-done.1.other_ref = bf16[1024,384]{1,0:T(8,128)(2,1)S(1)} collective-permute-done((bf16[1024,384]{1,0:T(8,128)(2,1)S(1)}, bf16[1024,384]{1,0:T(8,128)(2,1)S(1)}, u32[]{:S(2)}, u32[]{:S(2)}) %collective-permute-start.1) | collective-permute-done | bytes 786464 | tf_op jit(solution)/shard_map/ppermute | solution.py:426
  45.0 0.0 copy-done.4
  45.0 8.7 %shard_map.87 = (bf16[640,4096]{1,0:T(8,128)(2,1)S(1)}, f32[16,1,768]{2,1,0:T(1,128)S(1)}, f32[1,640]{1,0:T(1,128)S(1)}, f32[1,4096]{1,0:T(1,128)S(1)}) custom-call(s32[1]{0:T(128)} %bitcast.core_ref, s32[2]{0:T(128)S(1)} %copy-done.4, bf16[1024,384]{1,0:T(8,128)(2,1)S(1)} %bitcast.13, bf16[1024,384]{1,0:T(8,128)(2,1)S(1)} %collective-permute-done.1.other_ref, ...), custom_call_target="tpu_custom_call" | custom-call | tf_op jit(solution)/shard_map/pallas_call | solution.py:428
  53.7 26.2 %all_to_all.31.got_ref = f32[16,1,768]{2,1,0:T(1,128)S(1)} all-to-all(f32[16,1,768]{2,1,0:T(1,128)S(1)} %get-tuple-element.29), channel_id=1, replica_groups={{0,2,4,6,8,10,12,14,16,18,20,22,24,26,28,30},{1,3,5,7,9,11,13,15,17,19,..., dimensions={0} | all-to-all | bytes 98304 | tf_op jit(solution)/shard_map/all_to_all | solution.py:377
  79.9 2.8 %shard_map.88 = (f32[16,1,640]{2,1,0:T(1,128)S(1)}, f32[1,640]{1,0:T(1,128)S(1)}, f32[1,640]{1,0:T(1,128)S(1)}, f32[1,4096]{1,0:T(1,128)S(1)}, f32[1,2048]{1,0:T(1,128)S(1)}, /*index=5*/f32[1,2048]{1,0:T(1,128)S(1)}) custom-call(s32[1]{0:T(128)} %bitcast.core_ref, s32[2]{0:T(128)S(1)} %copy-done.4, f32[16,1,768]{2,1,0:T(1,128)S(1)} %all_to_all.31.got_ref, ...), custom_call_target="tpu_custom_call" | custom-call | tf_op jit(solution)/shard_map/pallas_call | solution.py:450
  82.7 14.0 %all_to_all.32.got_ref = f32[16,1,640]{2,1,0:T(1,128)S(1)} all-to-all(f32[16,1,640]{2,1,0:T(1,128)S(1)} %get-tuple-element.33), channel_id=1, replica_groups={{0,2,4,6,8,10,12,14,16,18,20,22,24,26,28,30},{1,3,5,7,9,11,13,15,17,19,..., dimensions={0} | all-to-all | bytes 81920 | tf_op jit(solution)/shard_map/all_to_all | solution.py:377
  96.8 1.4 %shard_map.89 = (f32[32,1,2048]{2,1,0:T(1,128)S(1)}, f32[1,2688]{1,0:T(1,128)S(1)}) custom-call(s32[1]{0:T(128)} %bitcast.core_ref, s32[2]{0:T(128)S(1)} %copy-done.4, f32[16,1,640]{2,1,0:T(1,128)S(1)} %all_to_all.32.got_ref, f32[1,640]{1,0:T(1,128)S(1)} %get-tuple-element.34.scale_ref, f32[1,640]{1,0:T(1,128)S(1)} %get-tuple-element.35.base_ref, ...), custom_call_target="tpu_custom_call" | custom-call | tf_op jit(solution)/shard_map/pallas_call | solution.py:464
  98.2 15.0 %all_to_all.33.refs_0_ = f32[32,1,2048]{2,1,0:T(1,128)S(1)} all-to-all(f32[32,1,2048]{2,1,0:T(1,128)S(1)} %get-tuple-element.42), channel_id=1, replica_groups={{0,1,32,33,64,65,96,97,128,129,160,161,192,193,224,225,256,257,288,289,..., dimensions={0} | all-to-all | bytes 524288 | tf_op jit(solution)/shard_map/all_to_all | solution.py:377
  113.1 0.8 shard_map.91
  114.0 3.6 %all-to-all-start.5 = ((f32[32,1,128]{2,1,0:T(1,128)}), f32[32,1,128]{2,1,0:T(1,128)S(1)}, u32[]{:S(2)}, u32[]{:S(2)}) async-start(f32[32,1,128]{2,1,0:T(1,128)} %get-tuple-element.43), calls=%async_computation.5 | async-start | bytes 32768 | tf_op jit(solution)/shard_map/all_to_all | solution.py:377
  117.6 2.3 %collective-permute-start.3 = (f32[1,2688]{1,0:T(1,128)S(1)}, f32[1,2688]{1,0:T(1,128)S(1)}, u32[]{:S(2)}, u32[]{:S(2)}) collective-permute-start(f32[1,2688]{1,0:T(1,128)S(1)} %get-tuple-element.38.pass_ref), channel_id=1, source_target_pairs={{0,1},{1,0},{2,3},{3,2},{4,5},{5,4},{6,7},{7,6},{8,9},{9,8},{10,11... | collective-permute-start | bytes 32264 | tf_op jit(solution)/shard_map/ppermute | solution.py:471
  119.9 0.8 collective-permute-done.3.back_ref
  120.7 0.7 shard_map.90
  121.4 8.1 %all-to-all-done.5.got_ref = f32[32,1,128]{2,1,0:T(1,128)S(1)} async-done(((f32[32,1,128]{2,1,0:T(1,128)}), f32[32,1,128]{2,1,0:T(1,128)S(1)}, u32[]{:S(2)}, u32[]{:S(2)}) %all-to-all-start.5) | async-done | bytes 16416 | tf_op jit(solution)/shard_map/all_to_all | solution.py:377
  129.5 0.8 shard_map.92
Async XLA Ops:
  0.6 0.7 copy-start.2
  1.3 0.7 copy-start.3
  4.1 21.8 %copy-start = (bf16[2048,300]{0,1:T(8,128)(2,1)S(1)}, bf16[2048,300]{0,1:T(8,128)(2,1)}, u32[]{:S(2)}) copy-start(bf16[2048,300]{0,1:T(8,128)(2,1)} %param.7) | copy-start | bytes 3686404
  4.1 26.8 %copy-start.1 = (f32[2048]{0:T(1024)S(1)}, f32[2048]{0:T(1024)}, u32[]{:S(2)}) copy-start(f32[2048]{0:T(1024)} %param.8) | copy-start | bytes 24580
  4.1 40.9 %copy-start.4 = (s32[2]{0:T(128)S(1)}, s32[2]{0:T(128)}, u32[]{:S(2)}) copy-start(s32[2]{0:T(128)} %count_ref.5) | copy-start | bytes 28
  22.3 15.3 %all-to-all-start.1 = ((bf16[16,64,384]{2,1,0:T(8,128)(2,1)}), bf16[16,64,384]{2,1,0:T(8,128)(2,1)S(1)}, u32[]{:S(2)}, u32[]{:S(2)}) async-start(bf16[16,64,384]{2,1,0:T(8,128)(2,1)} %bitcast.4), calls=%async_computation.1 | async-start | bytes 1572864 | tf_op jit(solution)/shard_map/all_to_all | solution.py:377
  25.9 17.2 %collective-permute-start.2 = (bf16[300,2048]{1,0:T(8,128)(2,1)S(1)}, bf16[300,2048]{1,0:T(8,128)(2,1)S(1)}, u32[]{:S(2)}, u32[]{:S(2)}) collective-permute-start(bf16[300,2048]{1,0:T(8,128)(2,1)S(1)} %bitcast.9), channel_id=1, source_target_pairs={{0,1},{1,0},{2,3},{3,2},{4,5},{5,4},{6,7},{7,6},{8,9},{9,8},{10,11... | collective-permute-start | bytes 3686408 | tf_op jit(solution)/shard_map/ppermute | solution.py:410
  31.0 3.1 %collective-permute-start = (f32[1,2048]{1,0:T(1,128)S(1)}, f32[1,2048]{1,0:T(1,128)S(1)}, u32[]{:S(2)}, u32[]{:S(2)}) collective-permute-start(f32[1,2048]{1,0:T(1,128)S(1)} %bitcast.14), channel_id=1, source_target_pairs={{0,1},{1,0},{2,3},{3,2},{4,5},{5,4},{6,7},{7,6},{8,9},{9,8},{10,11... | collective-permute-start | bytes 24584 | tf_op jit(solution)/shard_map/ppermute | solution.py:412
  37.6 7.4 %collective-permute-start.1 = (bf16[1024,384]{1,0:T(8,128)(2,1)S(1)}, bf16[1024,384]{1,0:T(8,128)(2,1)S(1)}, u32[]{:S(2)}, u32[]{:S(2)}) collective-permute-start(bf16[1024,384]{1,0:T(8,128)(2,1)S(1)} %bitcast.12), channel_id=1, source_target_pairs={{0,1},{1,0},{2,3},{3,2},{4,5},{5,4},{6,7},{7,6},{8,9},{9,8},{10,11... | collective-permute-start | bytes 2359304 | tf_op jit(solution)/shard_map/ppermute | solution.py:426
  114.0 15.6 %all-to-all-start.5 = ((f32[32,1,128]{2,1,0:T(1,128)}), f32[32,1,128]{2,1,0:T(1,128)S(1)}, u32[]{:S(2)}, u32[]{:S(2)}) async-start(f32[32,1,128]{2,1,0:T(1,128)} %get-tuple-element.43), calls=%async_computation.5 | async-start | bytes 32768 | tf_op jit(solution)/shard_map/all_to_all | solution.py:377
  117.6 3.1 %collective-permute-start.3 = (f32[1,2688]{1,0:T(1,128)S(1)}, f32[1,2688]{1,0:T(1,128)S(1)}, u32[]{:S(2)}, u32[]{:S(2)}) collective-permute-start(f32[1,2688]{1,0:T(1,128)S(1)} %get-tuple-element.38.pass_ref), channel_id=1, source_target_pairs={{0,1},{1,0},{2,3},{3,2},{4,5},{5,4},{6,7},{7,6},{8,9},{9,8},{10,11... | collective-permute-start | bytes 32264 | tf_op jit(solution)/shard_map/ppermute | solution.py:471
